TPU v7x, 32 devices: a whole 2x2x4 slice. The times are simulated.
32 devices in a mesh: dp: 4 (over z), zero: 8 (over y, x, core).
Axes of the slice: x: 2, y: 2, z: 4, core: 2. Of those that a mesh axis runs over, the one named last changes fastest.
Arguments:
- block_input: float32 [4, 1024, 1024], P('dp', 'zero'), may hold values from -6 to 6
- out_cotangent: float32 [4, 1024, 1024], P('dp', 'zero'), may hold values from -6 to 6
- segment_ids: int32 [4, 1024], P('dp'), may hold values from 0 to 3, never falling along the last dimension, each value on 1 to 512 neighbouring positions
- query_key_value_weight: float32 [1024, 4096], P(('dp', 'zero')), may hold values from -0.1875 to 0.1875
- w_out: float32 [2048, 1024], P(('dp', 'zero')), may hold values from -1 to 1
- w_gateup: float32 [1024, 6144], P(('dp', 'zero')), may hold values from -0.1875 to 0.1875
- w_down: float32 [3072, 1024], P(('dp', 'zero')), may hold values from -0.109375 to 0.109375
- norm_gains: float32 [1024, 2], P(('dp', 'zero')), may hold values from 0.5 to 1.5
- head_gains: float32 [128, 2], P(('dp', 'zero')), may hold values from 0.5 to 2.4, as said below
- first_moment_projection: float32 [1024, 4096], P(('dp', 'zero')), may hold values from -96 to 96
- mean_out: float32 [2048, 1024], P(('dp', 'zero')), may hold values from -19.2 to 19.2
- mean_gateup: float32 [1024, 6144], P(('dp', 'zero')), may hold values from -19.2 to 19.2
- mean_down: float32 [3072, 1024], P(('dp', 'zero')), may hold values from -19.2 to 19.2
- mean_norms: float32 [1024, 2], P(('dp', 'zero')), may hold values from -153.6 to 153.6
- mean_heads: float32 [128, 2], P(('dp', 'zero')), may hold values from -96 to 96
- second_moment_projection: float32 [1024, 4096], P(('dp', 'zero')), may hold values from 245.76 to 2457.6
- square_out: float32 [2048, 1024], P(('dp', 'zero')), may hold values from 8.192 to 81.92
- square_gateup: float32 [1024, 6144], P(('dp', 'zero')), may hold values from 8.192 to 81.92
- square_down: float32 [3072, 1024], P(('dp', 'zero')), may hold values from 8.192 to 81.92
- square_norms: float32 [1024, 2], P(('dp', 'zero')), may hold values from 409.6 to 4096
- square_heads: float32 [128, 2], P(('dp', 'zero')), may hold values from 204.8 to 2048
Outputs:
- block_output: float32 [4, 1024, 1024], P('dp', 'zero')
- input_grad: float32 [4, 1024, 1024], P('dp', 'zero')
- grad_qkv: float32 [1024, 4096], P(('dp', 'zero'))
- grad_out: float32 [2048, 1024], P(('dp', 'zero'))
- grad_gateup: float32 [1024, 6144], P(('dp', 'zero'))
- grad_down: float32 [3072, 1024], P(('dp', 'zero'))
- grad_norms: float32 [1024, 2], P(('dp', 'zero'))
- grad_heads: float32 [128, 2], P(('dp', 'zero'))
- next_qkv: float32 [1024, 4096], P(('dp', 'zero'))
- next_out: float32 [2048, 1024], P(('dp', 'zero'))
- next_gateup: float32 [1024, 6144], P(('dp', 'zero'))
- next_down: float32 [3072, 1024], P(('dp', 'zero'))
- next_norms: float32 [1024, 2], P(('dp', 'zero'))
- next_heads: float32 [128, 2], P(('dp', 'zero'))
- next_mean_qkv: float32 [1024, 4096], P(('dp', 'zero'))
- next_mean_out: float32 [2048, 1024], P(('dp', 'zero'))
- next_mean_gateup: float32 [1024, 6144], P(('dp', 'zero'))
- next_mean_down: float32 [3072, 1024], P(('dp', 'zero'))
- next_mean_norms: float32 [1024, 2], P(('dp', 'zero'))
- next_mean_heads: float32 [128, 2], P(('dp', 'zero'))
- next_square_qkv: float32 [1024, 4096], P(('dp', 'zero'))
- next_square_out: float32 [2048, 1024], P(('dp', 'zero'))
- next_square_gateup: float32 [1024, 6144], P(('dp', 'zero'))
- next_square_down: float32 [3072, 1024], P(('dp', 'zero'))
- next_square_norms: float32 [1024, 2], P(('dp', 'zero'))
- next_square_heads: float32 [128, 2], P(('dp', 'zero'))
Inputs may be any that keep to these rules, and one draw needn't show every extreme that they name: `segment_ids`: along each sequence the number never falls; each of the 4 documents has 1 to 512 tokens, one exactly 512. `head_gains`: positive gains.
All inputs are finite; a program needn't handle non-finite values.
Results may differ from a plain program's by a relative error of at most 0.04.
Values may be sent and summed in bfloat16 or wider, within the bound.
No kernel may reach another device: no remote copies, remote signals or barrier semaphores. Data moves between devices by JAX's collectives and lax.ppermute only.
A program may use at most 192 MiB of HBM per device.

v0:
```python
import jax
import jax.numpy as jnp
from jax import lax
from jax.sharding import PartitionSpec as P

QUERY_HEADS = 16
KEY_VALUE_HEADS = 8
HEAD_SIZE = 128
FF = 3072


norm_eps = 1e-06
rope_base = 1000000.0
beta_one = 0.9
beta_two = 0.95
adam_eps = 1e-08
learn_rate = 0.01
decay_rate = 0.1
step_count = 3
score_masked = -1e30


def rotate_half(value):
    half = value.shape[-1] // 2
    return jnp.concatenate([-value[..., half:], value[..., :half]], axis=-1)


def rotate_back(value):
    half = value.shape[-1] // 2
    return jnp.concatenate([value[..., half:], -value[..., :half]], axis=-1)


def rope_tables(positions, width):
    steps_half = jnp.arange(width // 2, dtype=jnp.float32)
    frequency = rope_base ** (-(steps_half * 2.0 / width))
    angles = positions.astype(jnp.float32)[:, None] * frequency[None, :]
    angles = jnp.concatenate([angles, angles], axis=-1)
    return (jnp.cos(angles), jnp.sin(angles))


def rms_scale(value):
    return lax.rsqrt(jnp.mean(value * value, axis=-1, keepdims=True) + norm_eps)


def rms_back(grad_scaled, value, scale):
    normed = value * scale
    return scale * (grad_scaled - normed * jnp.mean(grad_scaled * normed, axis=-1, keepdims=True))


def adam_update(weight, grad, first, second):
    first_new = beta_one * first + (1.0 - beta_one) * grad
    second_new = beta_two * second + (1.0 - beta_two) * grad * grad
    first_hat = first_new / (1.0 - beta_one**step_count)
    second_hat = second_new / (1.0 - beta_two**step_count)
    weight_new = weight - learn_rate * (
        first_hat / (jnp.sqrt(second_hat) + adam_eps) + decay_rate * weight
    )
    return (weight_new, first_new, second_new)


def on_device(
    block_input,
    out_cotangent,
    segment_ids,
    query_key_value_weight,
    w_out,
    w_gateup,
    w_down,
    norm_gains,
    head_gains,
    first_moment_projection,
    mean_out,
    mean_gateup,
    mean_down,
    mean_norms,
    mean_heads,
    second_moment_projection,
    square_out,
    square_gateup,
    square_down,
    square_norms,
    square_heads,
):
    masters = (query_key_value_weight, w_out, w_gateup, w_down, norm_gains, head_gains)
    means = (first_moment_projection, mean_out, mean_gateup, mean_down, mean_norms, mean_heads)
    squares = (
        second_moment_projection,
        square_out,
        square_gateup,
        square_down,
        square_norms,
        square_heads,
    )
    low_qkv = query_key_value_weight.astype(jnp.bfloat16)
    low_out = w_out.astype(jnp.bfloat16)
    low_gateup = w_gateup.astype(jnp.bfloat16)
    low_down = w_down.astype(jnp.bfloat16)
    low_norms = norm_gains.astype(jnp.bfloat16)
    low_heads = head_gains.astype(jnp.bfloat16)
    collected = (
        lax.all_gather(low_qkv, ("dp", "zero"), axis=0, tiled=True),
        lax.all_gather(low_out, ("dp", "zero"), axis=0, tiled=True),
        lax.all_gather(low_gateup, ("dp", "zero"), axis=0, tiled=True),
        lax.all_gather(low_down, ("dp", "zero"), axis=0, tiled=True),
        lax.all_gather(low_norms, ("dp", "zero"), axis=0, tiled=True),
        lax.all_gather(low_heads, ("dp", "zero"), axis=0, tiled=True),
    )
    qkv_weight, out_weight, gateup_weight, down_weight, gains, heads = collected
    inputs = block_input[0]
    cotangent = out_cotangent[0]
    segments = segment_ids[0]
    token_rows = inputs.shape[0]
    sequence_length = segments.shape[0]
    head_group = QUERY_HEADS // KEY_VALUE_HEADS
    query_span_width = QUERY_HEADS * HEAD_SIZE
    key_span_width = KEY_VALUE_HEADS * HEAD_SIZE
    score_scale = HEAD_SIZE ** (-0.5)
    first_row = lax.axis_index("zero") * token_rows
    last_row = first_row + token_rows - 1
    positions = first_row + jnp.arange(token_rows, dtype=jnp.int32)
    query_segments = lax.dynamic_slice_in_dim(segments, first_row, token_rows)
    cosine, sine = rope_tables(positions, HEAD_SIZE)
    cosine = cosine[:, None, :]
    sine = sine[:, None, :]
    gain_one = gains[:, 0].astype(jnp.float32)
    gain_two = gains[:, 1].astype(jnp.float32)
    query_gain = heads[:, 0].astype(jnp.float32)
    key_gain = heads[:, 1].astype(jnp.float32)
    scale_one = rms_scale(inputs)
    normed_input = (inputs * scale_one * gain_one).astype(jnp.bfloat16)
    projected_output = jnp.dot(normed_input, qkv_weight, preferred_element_type=jnp.float32)
    query = projected_output[:, :query_span_width].reshape(token_rows, QUERY_HEADS, HEAD_SIZE)
    key = projected_output[:, query_span_width : query_span_width + key_span_width].reshape(
        token_rows, KEY_VALUE_HEADS, HEAD_SIZE
    )
    value_local = projected_output[:, query_span_width + key_span_width :].astype(jnp.bfloat16)
    query_scale = rms_scale(query)
    key_scale = rms_scale(key)
    query_normed = query * query_scale * query_gain
    key_normed = key * key_scale * key_gain
    rotated_queries = (query_normed * cosine + rotate_half(query_normed) * sine).astype(
        jnp.bfloat16
    )
    key_turned = (
        (key_normed * cosine + rotate_half(key_normed) * sine)
        .astype(jnp.bfloat16)
        .reshape(token_rows, key_span_width)
    )
    grouped_queries = rotated_queries.reshape(token_rows, KEY_VALUE_HEADS, head_group, HEAD_SIZE)

    def block_mask(key_start, running_count):
        key_positions = key_start + jnp.arange(running_count, dtype=jnp.int32)
        key_segments = lax.dynamic_slice_in_dim(segments, key_start, running_count)
        same_doc = query_segments[:, None] == key_segments[None, :]
        return same_doc & (positions[:, None] >= key_positions[None, :])

    initial = (
        jnp.full((KEY_VALUE_HEADS, head_group, token_rows), score_masked, jnp.float32),
        jnp.zeros((KEY_VALUE_HEADS, head_group, token_rows), jnp.float32),
        jnp.zeros((KEY_VALUE_HEADS, head_group, token_rows, HEAD_SIZE), jnp.float32),
    )
    block_number = min(512, sequence_length)
    block_count = sequence_length // block_number
    block_keys = lax.all_gather(key_turned, "zero", axis=0, tiled=True)
    block_values = lax.all_gather(value_local, "zero", axis=0, tiled=True)
    key_start = jnp.int32(0)
    running_count = block_keys.shape[0]

    def attend_live(carried):
        top, total, accum = carried
        keys_threefold = block_keys.reshape(running_count, KEY_VALUE_HEADS, HEAD_SIZE)
        values_threefold = block_values.reshape(running_count, KEY_VALUE_HEADS, HEAD_SIZE)
        allowed = block_mask(key_start, running_count)
        scores = (
            jnp.einsum(
                "tgrd,kgd->grtk",
                grouped_queries,
                keys_threefold,
                preferred_element_type=jnp.float32,
            )
            * score_scale
        )
        scores = jnp.where(allowed, scores, score_masked)
        new_top = jnp.maximum(top, jnp.max(scores, axis=-1))
        weights = jnp.where(allowed, jnp.exp(scores - new_top[..., None]), 0.0)
        new_total = jnp.sum(weights, axis=-1)
        added = jnp.einsum(
            "grtk,kgd->grtd",
            weights.astype(jnp.bfloat16),
            values_threefold,
            preferred_element_type=jnp.float32,
        )
        return (new_top, new_total, added)

    top, total, accum = lax.cond(
        key_start <= last_row, attend_live, lambda carried: carried, initial
    )
    every_key, every_value = (
        lax.all_gather(key_turned, "zero", axis=0, tiled=True),
        lax.all_gather(value_local, "zero", axis=0, tiled=True),
    )
    log_total = top + jnp.log(total)
    attention_output = (
        jnp.transpose(accum / total[..., None], (2, 0, 1, 3))
        .reshape(token_rows, query_span_width)
        .astype(jnp.bfloat16)
    )
    middle = inputs + jnp.dot(attention_output, out_weight, preferred_element_type=jnp.float32)
    scale_two = rms_scale(middle)
    normed_mid = (middle * scale_two * gain_two).astype(jnp.bfloat16)
    gateup = jnp.dot(normed_mid, gateup_weight, preferred_element_type=jnp.float32)
    gate = gateup[:, :FF]
    upward = gateup[:, FF:]
    sigma = jax.nn.sigmoid(gate)
    hidden = (gate * sigma * upward).astype(jnp.bfloat16)
    output = middle + jnp.dot(hidden, down_weight, preferred_element_type=jnp.float32)
    cot_low = cotangent.astype(jnp.bfloat16)
    grad_down = jnp.einsum("tf,td->fd", hidden, cot_low, preferred_element_type=jnp.float32)
    grad_hidden = jnp.einsum("td,fd->tf", cot_low, down_weight, preferred_element_type=jnp.float32)
    gate_term = grad_hidden * upward * sigma * (1.0 + gate * (1.0 - sigma))
    up_term = grad_hidden * gate * sigma
    gateup_grad = jnp.concatenate([gate_term, up_term], axis=-1).astype(jnp.bfloat16)
    grad_gateup = jnp.einsum(
        "td,tf->df", normed_mid, gateup_grad, preferred_element_type=jnp.float32
    )
    grad_normed_mid = jnp.einsum(
        "tf,df->td", gateup_grad, gateup_weight, preferred_element_type=jnp.float32
    )
    grad_gain_two = jnp.sum(grad_normed_mid * middle * scale_two, axis=0)
    grad_middle = cotangent + rms_back(grad_normed_mid * gain_two, middle, scale_two)
    middle_low = grad_middle.astype(jnp.bfloat16)
    grad_out = jnp.einsum(
        "tq,td->qd", attention_output, middle_low, preferred_element_type=jnp.float32
    )
    attention_output_gradient = jnp.einsum(
        "td,qd->tq", middle_low, out_weight, preferred_element_type=jnp.float32
    ).astype(jnp.bfloat16)
    grouped_gradient = attention_output_gradient.reshape(
        token_rows, KEY_VALUE_HEADS, head_group, HEAD_SIZE
    )
    grouped_attention_output = attention_output.reshape(
        token_rows, KEY_VALUE_HEADS, head_group, HEAD_SIZE
    )
    output_difference = jnp.einsum(
        "mhln,mhln->hlm",
        grouped_gradient,
        grouped_attention_output,
        preferred_element_type=jnp.float32,
    )

    def back_block(grad_query, index):
        start_offset = index * block_number
        block_keys = lax.dynamic_slice_in_dim(every_key, start_offset, block_number).reshape(
            block_number, KEY_VALUE_HEADS, HEAD_SIZE
        )
        block_values = lax.dynamic_slice_in_dim(every_value, start_offset, block_number).reshape(
            block_number, KEY_VALUE_HEADS, HEAD_SIZE
        )

        def back_live(carried):
            allowed = block_mask(start_offset, block_number)
            scores = (
                jnp.einsum(
                    "tgrd,kgd->grtk",
                    grouped_queries,
                    block_keys,
                    preferred_element_type=jnp.float32,
                )
                * score_scale
            )
            soft = jnp.where(allowed, jnp.exp(scores - log_total[..., None]), 0.0)
            soft_low = soft.astype(jnp.bfloat16)
            value_term = jnp.einsum(
                "grtk,tgrd->kgd", soft_low, grouped_gradient, preferred_element_type=jnp.float32
            )
            grad_soft = jnp.einsum(
                "tgrd,kgd->grtk", grouped_gradient, block_values, preferred_element_type=jnp.float32
            )
            grad_scores = (soft * (grad_soft - output_difference[..., None])).astype(jnp.bfloat16)
            new_query = carried + jnp.einsum(
                "grtk,kgd->tgrd", grad_scores, block_keys, preferred_element_type=jnp.float32
            )
            key_term = (
                jnp.einsum(
                    "grtk,tgrd->kgd",
                    grad_scores,
                    grouped_queries,
                    preferred_element_type=jnp.float32,
                )
                * score_scale
            )
            return (
                new_query,
                key_term.reshape(block_number, key_span_width),
                value_term.reshape(block_number, key_span_width),
            )

        def skipped(carried):
            empty = jnp.zeros((block_number, key_span_width), jnp.float32)
            return (carried, empty, empty)

        new_query, key_term, value_term = lax.cond(
            start_offset <= last_row, back_live, skipped, grad_query
        )
        return (new_query, (key_term, value_term))

    grad_query, (key_terms, value_terms) = lax.scan(
        back_block,
        jnp.zeros((token_rows, KEY_VALUE_HEADS, head_group, HEAD_SIZE), jnp.float32),
        jnp.arange(block_count, dtype=jnp.int32),
    )
    key_terms = key_terms.reshape(sequence_length, key_span_width)
    value_terms = value_terms.reshape(sequence_length, key_span_width)
    key_gradient, grad_value = (
        lax.psum_scatter(
            key_terms.astype(jnp.bfloat16), "zero", scatter_dimension=0, tiled=True
        ).astype(jnp.float32),
        lax.psum_scatter(
            value_terms.astype(jnp.bfloat16), "zero", scatter_dimension=0, tiled=True
        ).astype(jnp.float32),
    )
    grad_query = grad_query.reshape(token_rows, QUERY_HEADS, HEAD_SIZE) * score_scale
    key_gradient = key_gradient.reshape(token_rows, KEY_VALUE_HEADS, HEAD_SIZE)
    grad_query_normed = grad_query * cosine + rotate_back(grad_query * sine)
    grad_key_normed = key_gradient * cosine + rotate_back(key_gradient * sine)
    grad_query_gain = jnp.sum(grad_query_normed * query * query_scale, axis=(0, 1))
    grad_key_gain = jnp.sum(grad_key_normed * key * key_scale, axis=(0, 1))
    grad_query_pre = rms_back(grad_query_normed * query_gain, query, query_scale)
    grad_key_pre = rms_back(grad_key_normed * key_gain, key, key_scale)
    grad_projected = jnp.concatenate(
        [
            grad_query_pre.reshape(token_rows, query_span_width),
            grad_key_pre.reshape(token_rows, key_span_width),
            grad_value,
        ],
        axis=-1,
    ).astype(jnp.bfloat16)
    grad_qkv = jnp.einsum(
        "td,tf->df", normed_input, grad_projected, preferred_element_type=jnp.float32
    )
    grad_normed_input = jnp.einsum(
        "tf,df->td", grad_projected, qkv_weight, preferred_element_type=jnp.float32
    )
    grad_gain_one = jnp.sum(grad_normed_input * inputs * scale_one, axis=0)
    grad_input = grad_middle + rms_back(grad_normed_input * gain_one, inputs, scale_one)
    grad_norms = jnp.stack([grad_gain_one, grad_gain_two], axis=1)
    grad_heads = jnp.stack([grad_query_gain, grad_key_gain], axis=1)
    summed = (
        lax.psum_scatter(grad_qkv, ("dp", "zero"), scatter_dimension=0, tiled=True),
        lax.psum_scatter(grad_out, ("dp", "zero"), scatter_dimension=0, tiled=True),
        lax.psum_scatter(grad_gateup, ("dp", "zero"), scatter_dimension=0, tiled=True),
        lax.psum_scatter(grad_down, ("dp", "zero"), scatter_dimension=0, tiled=True),
        lax.psum_scatter(grad_norms, ("dp", "zero"), scatter_dimension=0, tiled=True),
        lax.psum_scatter(grad_heads, ("dp", "zero"), scatter_dimension=0, tiled=True),
    )
    updated = [
        adam_update(masters[index], summed[index], means[index], squares[index])
        for index in range(6)
    ]
    return (
        output[None],
        grad_input[None],
        summed[0],
        summed[1],
        summed[2],
        summed[3],
        summed[4],
        summed[5],
        updated[0][0],
        updated[1][0],
        updated[2][0],
        updated[3][0],
        updated[4][0],
        updated[5][0],
        updated[0][1],
        updated[1][1],
        updated[2][1],
        updated[3][1],
        updated[4][1],
        updated[5][1],
        updated[0][2],
        updated[1][2],
        updated[2][2],
        updated[3][2],
        updated[4][2],
        updated[5][2],
    )


def solution(mesh):
    placed = (
        P("dp", "zero", None),
        P("dp", "zero", None),
        P("dp", None),
        P(("dp", "zero"), None),
        P(("dp", "zero"), None),
        P(("dp", "zero"), None),
        P(("dp", "zero"), None),
        P(("dp", "zero"), None),
        P(("dp", "zero"), None),
        P(("dp", "zero"), None),
        P(("dp", "zero"), None),
        P(("dp", "zero"), None),
        P(("dp", "zero"), None),
        P(("dp", "zero"), None),
        P(("dp", "zero"), None),
        P(("dp", "zero"), None),
        P(("dp", "zero"), None),
        P(("dp", "zero"), None),
        P(("dp", "zero"), None),
        P(("dp", "zero"), None),
        P(("dp", "zero"), None),
    )
    return jax.shard_map(
        on_device,
        mesh=mesh,
        in_specs=placed,
        out_specs=(
            P("dp", "zero", None),
            P("dp", "zero", None),
            P(("dp", "zero"), None),
            P(("dp", "zero"), None),
            P(("dp", "zero"), None),
            P(("dp", "zero"), None),
            P(("dp", "zero"), None),
            P(("dp", "zero"), None),
            P(("dp", "zero"), None),
            P(("dp", "zero"), None),
            P(("dp", "zero"), None),
            P(("dp", "zero"), None),
            P(("dp", "zero"), None),
            P(("dp", "zero"), None),
            P(("dp", "zero"), None),
            P(("dp", "zero"), None),
            P(("dp", "zero"), None),
            P(("dp", "zero"), None),
            P(("dp", "zero"), None),
            P(("dp", "zero"), None),
            P(("dp", "zero"), None),
            P(("dp", "zero"), None),
            P(("dp", "zero"), None),
            P(("dp", "zero"), None),
            P(("dp", "zero"), None),
            P(("dp", "zero"), None),
        ),
        check_vma=False,
    )
```

profile of v0, /device:TPU:0, one launch (start us, length us, event | category | flops | bytes accessed | tf_op | source)
XLA Modules:
  0.0 1421.2 jit_solution(5240921533018461196)
XLA Ops:
  7.2 1.8 convert_element_type.147
  9.8 43.3 %all-gather = bf16[32,32,2]{1,2,0:T(2,128)(2,1)S(1)} all-gather(bf16[1,32,2]{1,2,0:T(2,128)(2,1)S(1)} %convert_bitcast_fusion.2), channel_id=1, replica_groups=mesh['dp'=4,'zero'=8] {'dp','zero'}, dimensions={0}, use_global_device_ids=true | all-gather | bytes 4224 | tf_op jit(solution)/shard_map/all_gather | solution.py:105
  53.9 37.6 %all-gather.1 = bf16[32,4,2]{1,2,0:T(2,128)(2,1)S(1)} all-gather(bf16[1,4,2]{1,2,0:T(2,128)(2,1)S(1)} %convert_bitcast_fusion.1), channel_id=1, replica_groups=mesh['dp'=4,'zero'=8] {'dp','zero'}, dimensions={0}, use_global_device_ids=true | all-gather | bytes 528 | tf_op jit(solution)/shard_map/all_gather | solution.py:106
  92.7 1.2 fusion.50
  94.4 4.9 fusion.71
  104.1 1.6 convert_element_type.159
  110.7 1.4 copy.170
  112.1 1.4 fusion.34
  113.5 2.0 copy.173
  115.6 13.0 all-gather.11.cloned.1.call-done
  128.5 30.3 %all-gather.13.cloned.1.call-done = bf16[1024,1024]{1,0:T(8,128)(2,1)} async-done(((bf16[128,1024]{1,0:T(8,128)(2,1)}), bf16[1024,1024]{1,0:T(8,128)(2,1)}) %all-gather.13.cloned.1.call-update) | async-done | bytes 2097168 | tf_op jit(solution)/shard_map/all_gather | solution.py:165
  158.8 12.3 conditional.2
  159.0 2.2 copy.221
  161.2 1.4 fusion.2
  163.3 3.4 fusion.4
  168.0 3.0 fusion.5
  171.8 4.0 copy.172
  175.8 4.5 copy.174
  181.1 42.7 %all-gather.15.cloned.1.call-done = bf16[2048,1024]{1,0:T(8,128)(2,1)} async-done(((bf16[64,1024]{1,0:T(8,128)(2,1)}), bf16[2048,1024]{1,0:T(8,128)(2,1)}) %all-gather.15.cloned.1.call-update) | async-done | bytes 4194320 | tf_op jit(solution)/shard_map/all_gather | solution.py:102
  223.9 3.0 multiply_reduce_fusion.7
  226.9 94.2 %all-gather.17.cloned.1.call-done = bf16[1024,6144]{1,0:T(8,128)(2,1)} async-done(((bf16[32,6144]{1,0:T(8,128)(2,1)}), bf16[1024,6144]{1,0:T(8,128)(2,1)}) %all-gather.17.cloned.1.call-update) | async-done | bytes 12582928 | tf_op jit(solution)/shard_map/all_gather | solution.py:103
  321.1 8.0 fusion.72
  329.2 63.0 %all-gather.19.cloned.1.call-done = bf16[3072,1024]{1,0:T(8,128)(2,1)} async-done(((bf16[96,1024]{1,0:T(8,128)(2,1)}), bf16[3072,1024]{1,0:T(8,128)(2,1)}) %all-gather.19.cloned.1.call-update) | async-done | bytes 6291472 | tf_op jit(solution)/shard_map/all_gather | solution.py:104
  392.2 7.9 multiply_convert_fusion.1
  400.1 7.2 multiply_reduce_fusion.3
  407.3 1.5 bitcast_add_fusion.2
  409.7 3.7 convolution_convert_fusion
  414.1 1.2 copy.175
  416.8 14.2 %while.18 = (s32[]{:T(128)}, f32[128,8,2,128]{3,0,2,1:T(8,128)S(1)}, bf16[2,512,1024]{1,2,0:T(8,128)(2,1)}, bf16[2,512,1024]{1,2,0:T(8,128)(2,1)}, s32[2]{0:T(12...) while((s32[]{:T(128)}, ...), condition=%wide.region_12.13_spmd.clone, body=%wide.region_9.12_spmd.clone.sunk | while | flops 1354171008 | bytes 41129376 | solution.py:307
  418.3 8.4 conditional.5
  418.3 2.9 constant_dynamic-slice_fusion
  422.2 1.5 fusion.16
  424.5 1.2 fusion.26
  426.7 1.5 constant_dynamic-update-slice_fusion.3
  429.6 1.5 constant_dynamic-update-slice_fusion.3
  431.0 4.0 copy.183
  435.2 1.3 copy.182
  436.5 4.0 copy.184
  441.4 1.8 copy.176
  446.2 3.2 reshape.319
  449.4 1.8 pad_maximum_fusion.1
  452.2 2.4 multiply_reduce_fusion.1
  454.6 28.4 %reduce-scatter.11.cloned.1.call-done = bf16[128,1024]{1,0:T(8,128)(2,1)} async-done(((bf16[1024,1024]{1,0:T(8,128)(2,1)}), bf16[128,1024]{1,0:T(8,128)(2,1)}) %reduce-scatter.11.cloned.1.call-update) | async-done | bytes 262160 | tf_op jit(solution)/shard_map/reduce_scatter | solution.py:315
  482.9 1.0 convert_bitcast_fusion
  486.3 41.1 %reduce-scatter.13.cloned.1.call-done = bf16[128,1024]{1,0:T(8,128)(2,1)} async-done(((bf16[1024,1024]{1,0:T(8,128)(2,1)}), bf16[128,1024]{1,0:T(8,128)(2,1)}) %reduce-scatter.13.cloned.1.call-update) | async-done | bytes 262160 | tf_op jit(solution)/shard_map/reduce_scatter | solution.py:318
  527.4 7.3 fusion.52
  534.7 1.0 copy.215
  536.0 4.5 fusion.59
  540.6 1.1 copy-done.24
  541.8 6.4 fusion.84
  549.3 11.6 fusion.38
  561.8 8.2 fusion.53
  570.8 4.6 fusion.29
  575.5 39.4 %all-reduce = f32[128,2]{0,1:T(2,128)S(1)} all-reduce(f32[128,2]{0,1:T(2,128)S(1)} %pad_maximum_fusion.10), channel_id=9, replica_groups=mesh['dp'=4,'zero'=8] {'dp','zero'}, use_global_device_ids=true, to_apply=%region_29.30.clone | all-reduce | flops 256 | bytes 2048
  615.5 2.1 add_bitcast_fusion
  617.7 54.0 %reduce-scatter.23.cloned.1.call-done = f32[32,2]{1,0:T(8,128)} async-done(((f32[1024,2]{1,0:T(8,128)}), f32[32,2]{1,0:T(8,128)}) %reduce-scatter.23.cloned.1.call-update) | async-done | bytes 272
  673.1 147.3 %reduce-scatter.17.cloned.1.call-done = f32[64,1024]{1,0:T(8,128)} async-done(((f32[2048,1024]{1,0:T(8,128)}), f32[64,1024]{1,0:T(8,128)}) %reduce-scatter.17.cloned.1.call-update) | async-done | bytes 262160 | tf_op jit(solution)/shard_map/reduce_scatter | solution.py:350
  820.4 2.1 multiply_subtract_fusion.3
  822.5 155.2 %reduce-scatter.21.cloned.1.call-done = f32[96,1024]{1,0:T(8,128)} async-done(((f32[3072,1024]{1,0:T(8,128)}), f32[96,1024]{1,0:T(8,128)}) %reduce-scatter.21.cloned.1.call-update) | async-done | bytes 393232 | tf_op jit(solution)/shard_map/reduce_scatter | solution.py:352
  977.7 2.4 multiply_subtract_fusion.2
  980.1 246.5 %reduce-scatter.19.cloned.1.call-done = f32[32,6144]{1,0:T(8,128)} async-done(((f32[1024,6144]{1,0:T(8,128)}), f32[32,6144]{1,0:T(8,128)}) %reduce-scatter.19.cloned.1.call-update) | async-done | bytes 786448 | tf_op jit(solution)/shard_map/reduce_scatter | solution.py:351
  1226.7 3.1 multiply_subtract_fusion
  1229.8 182.2 %reduce-scatter.15.cloned.1.call-done = f32[32,4096]{1,0:T(8,128)} async-done(((f32[1024,4096]{1,0:T(8,128)}), f32[32,4096]{1,0:T(8,128)}) %reduce-scatter.15.cloned.1.call-update) | async-done | bytes 524304 | tf_op jit(solution)/shard_map/reduce_scatter | solution.py:349
  1412.0 2.4 multiply_subtract_fusion.1
  (238 shorter events, 36.4 us)
Async XLA Ops:
  7.2 87.2 %all-gather.9.cloned.1.call-start = ((), (), s32[]{:S(2)}) async-start(), calls=%async_computation.7 | async-start | bytes 8650752 | tf_op jit(solution)/shard_map/all_gather | solution.py:101
  9.0 119.5 %all-gather.11.cloned.1.call-start = ((), (), s32[]{:S(2)}) async-start(), calls=%async_computation.8 | async-start | bytes 2359296 | tf_op jit(solution)/shard_map/all_gather | solution.py:164
  93.8 5.5 copy-start.46
  94.4 5.4 copy-start.49
  99.3 8.5 copy-start.2
  100.8 4.9 copy-start.27
  101.3 5.4 copy-start.32
  102.2 5.5 copy-start.42
  103.2 55.6 %all-gather.13.cloned.1.call-start = ((), (), s32[]{:S(2)}) async-start(), calls=%async_computation.9 | async-start | bytes 2359296 | tf_op jit(solution)/shard_map/all_gather | solution.py:165
  104.0 119.8 %all-gather.15.cloned.1.call-start = ((), (), s32[]{:S(2)}) async-start(), calls=%async_computation.10 | async-start | bytes 4325376 | tf_op jit(solution)/shard_map/all_gather | solution.py:102
  105.7 215.4 %all-gather.17.cloned.1.call-start = ((), (), s32[]{:S(2)}) async-start(), calls=%async_computation.11 | async-start | bytes 12976128 | tf_op jit(solution)/shard_map/all_gather | solution.py:103
  106.6 285.6 %all-gather.19.cloned.1.call-start = ((), (), s32[]{:S(2)}) async-start(), calls=%async_computation.12 | async-start | bytes 6488064 | tf_op jit(solution)/shard_map/all_gather | solution.py:104
  107.4 375.6 %reduce-scatter.11.cloned.1.call-start = ((), (), s32[]{:S(2)}) async-start(), calls=%async_computation.13 | async-start | bytes 2359296 | tf_op jit(solution)/shard_map/reduce_scatter | solution.py:315
  107.9 1.4 copy-start.48
  109.1 3.0 copy-start.8
  158.8 2.4 copy-start.31
  163.3 4.2 copy-start.13
  171.1 9.2 copy-start.11
  175.8 48.1 %copy-start.4 = (f32[1,128,1024]{2,1,0:T(8,128)S(1)}, f32[1,128,1024]{2,1,0:T(8,128)}, u32[]{:S(2)}) copy-start(f32[1,128,1024]{2,1,0:T(8,128)} %param.27) | copy-start | bytes 1572868
  181.1 148.0 %copy-start.18 = (bf16[8,2,128,128]{2,3,1,0:T(8,128)(2,1)}, bf16[8,2,128,128]{2,3,1,0:T(8,128)(2,1)S(1)}, u32[]{:S(2)}) copy-start(bf16[8,2,128,128]{2,3,1,0:T(8,128)(2,1)S(1)} %divide_convert_fusion) | copy-start | bytes 1572868
  226.9 102.3 %copy-start.6 = (f32[128,1024]{1,0:T(8,128)}, f32[128,1024]{1,0:T(8,128)S(1)}, u32[]{:S(2)}) copy-start(f32[128,1024]{1,0:T(8,128)S(1)} %get-tuple-element.470) | copy-start | bytes 1572868
  226.9 180.4 %copy-start.44 = (f32[128]{0:T(128)}, f32[128]{0:T(128)S(1)}, u32[]{:S(2)}) copy-start(f32[128]{0:T(128)S(1)} %add_rsqrt_fusion.2) | copy-start | bytes 1540
  392.2 7.9 copy-start.1
  413.4 2.4 copy-start.12
  418.3 2.9 copy-start
  421.1 1.1 copy-start.39
  435.0 92.3 %reduce-scatter.13.cloned.1.call-start = ((), (), s32[]{:S(2)}) async-start(), calls=%async_computation.14 | async-start | bytes 2359296 | tf_op jit(solution)/shard_map/reduce_scatter | solution.py:318
  436.5 4.3 copy-start.41
  440.5 231.2 %reduce-scatter.23.cloned.1.call-start = ((), (), s32[]{:S(2)}) async-start(), calls=%async_computation.19 | async-start | bytes 540672
  443.5 2.6 copy-start.10
  443.5 1.6 copy-start.9
  449.4 2.2 copy-start.3
  449.4 2.4 copy-start.25
  449.4 2.8 copy-start.26
  454.6 29.8 %copy-start.50 = (f32[128]{0:T(128)S(1)}, f32[128]{0:T(128)}, u32[]{:S(2)}) copy-start(f32[128]{0:T(128)} %copy-done.49) | copy-start | bytes 1540
  484.0 1.0 copy-start.15
  484.1 1.5 copy-start.21
  484.1 1.5 copy-start.23
  484.1 1.5 copy-start.34
  484.6 42.8 %copy-start.5 = (f32[1,128,1024]{2,1,0:T(8,128)S(1)}, f32[1,128,1024]{2,1,0:T(8,128)}, u32[]{:S(2)}) copy-start(f32[1,128,1024]{2,1,0:T(8,128)} %param.27) | copy-start | bytes 1572868
  484.6 42.8 %copy-start.47 = (f32[128]{0:T(128)S(1)}, f32[128]{0:T(128)}, u32[]{:S(2)}) copy-start(f32[128]{0:T(128)} %copy-done.46) | copy-start | bytes 1540
  527.4 7.3 copy-start.52
  527.4 8.7 copy-start.17
  527.4 8.7 copy-start.19
  535.7 284.7 %reduce-scatter.17.cloned.1.call-start = ((), (), s32[]{:S(2)}) async-start(), calls=%async_computation.16 | async-start | bytes 8650752 | tf_op jit(solution)/shard_map/reduce_scatter | solution.py:350
  540.5 1.1 copy-start.24
  540.5 1.3 copy-start.30
  540.6 437.1 %reduce-scatter.21.cloned.1.call-start = ((), (), s32[]{:S(2)}) async-start(), calls=%async_computation.18 | async-start | bytes 12976128 | tf_op jit(solution)/shard_map/reduce_scatter | solution.py:352
  548.3 678.4 %reduce-scatter.19.cloned.1.call-start = ((), (), s32[]{:S(2)}) async-start(), calls=%async_computation.17 | async-start | bytes 25952256 | tf_op jit(solution)/shard_map/reduce_scatter | solution.py:351
  560.9 851.1 %reduce-scatter.15.cloned.1.call-start = ((), (), s32[]{:S(2)}) async-start(), calls=%async_computation.15 | async-start | bytes 17301504 | tf_op jit(solution)/shard_map/reduce_scatter | solution.py:349
  570.7 44.1 %copy-start.53 = (f32[4,2]{0,1:T(2,128)S(1)}, f32[4,2]{0,1:T(2,128)}, u32[]{:S(2)}) copy-start(f32[4,2]{0,1:T(2,128)} %param.35) | copy-start | bytes 100
  570.7 44.1 %copy-start.54 = (f32[4,2]{0,1:T(2,128)S(1)}, f32[4,2]{0,1:T(2,128)}, u32[]{:S(2)}) copy-start(f32[4,2]{0,1:T(2,128)} %param.41) | copy-start | bytes 100
  570.8 44.1 %copy-start.55 = (f32[4,2]{0,1:T(2,128)S(1)}, f32[4,2]{0,1:T(2,128)}, u32[]{:S(2)}) copy-start(f32[4,2]{0,1:T(2,128)} %param.47) | copy-start | bytes 100
  570.8 101.7 %copy-start.56 = (f32[32,2]{0,1:T(2,128)S(1)}, f32[32,2]{0,1:T(2,128)}, u32[]{:S(2)}) copy-start(f32[32,2]{0,1:T(2,128)} %param.34) | copy-start | bytes 772
  570.8 101.7 %copy-start.57 = (f32[32,2]{0,1:T(2,128)S(1)}, f32[32,2]{0,1:T(2,128)}, u32[]{:S(2)}) copy-start(f32[32,2]{0,1:T(2,128)} %param.40) | copy-start | bytes 772
  570.8 101.7 %copy-start.58 = (f32[32,2]{0,1:T(2,128)S(1)}, f32[32,2]{0,1:T(2,128)}, u32[]{:S(2)}) copy-start(f32[32,2]{0,1:T(2,128)} %param.46) | copy-start | bytes 772
  570.8 249.6 %copy-start.35 = (f32[64,1024]{1,0:T(8,128)S(1)}, f32[64,1024]{1,0:T(8,128)}, u32[]{:S(2)}) copy-start(f32[64,1024]{1,0:T(8,128)} %param.31) | copy-start | bytes 786436
  575.4 402.3 %copy-start.33 = (f32[96,1024]{1,0:T(8,128)S(1)}, f32[96,1024]{1,0:T(8,128)}, u32[]{:S(2)}) copy-start(f32[96,1024]{1,0:T(8,128)} %param.33) | copy-start | bytes 1179652
  615.5 611.1 %copy-start.28 = (f32[32,6144]{1,0:T(8,128)S(1)}, f32[32,6144]{1,0:T(8,128)}, u32[]{:S(2)}) copy-start(f32[32,6144]{1,0:T(8,128)} %param.32) | copy-start | bytes 2359300
  615.5 611.1 %copy-start.36 = (f32[32,6144]{1,0:T(8,128)S(1)}, f32[32,6144]{1,0:T(8,128)}, u32[]{:S(2)}) copy-start(f32[32,6144]{1,0:T(8,128)} %param.38) | copy-start | bytes 2359300
  672.5 557.3 %copy-start.51 = (f32[32,2]{0,1:T(2,128)}, f32[32,2]{0,1:T(2,128)S(1)}, u32[]{:S(2)}) copy-start(f32[32,2]{0,1:T(2,128)S(1)} %copy.216) | copy-start | bytes 772
  980.1 431.9 %copy-start.29 = (f32[32,4096]{1,0:T(8,128)S(1)}, f32[32,4096]{1,0:T(8,128)}, u32[]{:S(2)}) copy-start(f32[32,4096]{1,0:T(8,128)} %param.30) | copy-start | bytes 1572868
  980.1 431.9 %copy-start.37 = (f32[32,4096]{1,0:T(8,128)S(1)}, f32[32,4096]{1,0:T(8,128)}, u32[]{:S(2)}) copy-start(f32[32,4096]{1,0:T(8,128)} %param.36) | copy-start | bytes 1572868
  980.1 431.9 %copy-start.38 = (f32[32,4096]{1,0:T(8,128)S(1)}, f32[32,4096]{1,0:T(8,128)}, u32[]{:S(2)}) copy-start(f32[32,4096]{1,0:T(8,128)} %param.42) | copy-start | bytes 1572868
  (8 other events, 7.2 us)
Sparse Core Ops, SparseCore 0:
  11.4 79.8 all-gather.8
  103.3 25.1 all-gather.10
  131.0 27.7 all-gather.12
  162.1 61.7 all-gather.14
  227.1 93.9 all-gather.16
  324.4 67.7 all-gather.18
  435.2 47.7 reduce-scatter.10
  486.2 41.0 reduce-scatter.12
  535.8 135.7 reduce-scatter.22
  674.4 145.9 reduce-scatter.16
  827.0 150.6 reduce-scatter.20
  984.5 242.0 reduce-scatter.18
  1229.5 182.4 reduce-scatter.14
where the time goes:
time: 1430 us; the launch traced here: 1420 us
  waiting for transfers between devices  1100 us (77%)
  blocking collectives  120 us (8%)
  matrix products  87 us (6%)
  local copies, waits for them, and re-layouts  53.5 us (4%)
  other arithmetic  44.3 us (3%)
  between operations  15.1 us (1%)
    reduce_scatter x1, waiting for transfers between devices, on_device(): lax.psum_scatter(grad_gateup, ('dp', 'zero'), scatter_dimension=0, tiled=...  247 us
    reduce_scatter x1, waiting for transfers between devices, on_device(): lax.psum_scatter(grad_qkv, ('dp', 'zero'), scatter_dimension=0, tiled=True)  182 us
    reduce_scatter x1, waiting for transfers between devices, on_device(): lax.psum_scatter(grad_down, ('dp', 'zero'), scatter_dimension=0, tiled=True)  155 us
    reduce_scatter x1, waiting for transfers between devices, on_device(): lax.psum_scatter(grad_out, ('dp', 'zero'), scatter_dimension=0, tiled=True)  147 us
    all_gather x1, waiting for transfers between devices, on_device(): lax.all_gather(low_gateup, ('dp', 'zero'), axis=0, tiled=True)  94.2 us
    all_gather x1, waiting for transfers between devices, on_device(): lax.all_gather(low_down, ('dp', 'zero'), axis=0, tiled=True)  63 us
    unnamed x14, waiting for transfers between devices  54.2 us
    all_gather x1, blocking collectives, on_device(): lax.all_gather(low_norms, ('dp', 'zero'), axis=0, tiled=True)  43.3 us
  transfers between devices with their start and end apart: 13, of which 12 were waited for; matrix products, arithmetic and copies ran while one was open for 8% of the time, Pallas kernels for 0%

commit v1 on v0

--- a/solution.py
+++ b/solution.py
@@ -58,7 +58,7 @@
     return (weight_new, first_new, second_new)
 
 
-def on_device(
+def on_device_gathered(
     block_input,
     out_cotangent,
     segment_ids,
@@ -386,6 +386,420 @@
         updated[5][2],
     )
 
+def row_sum(value):
+    return jnp.sum(value, axis=1)
+
+
+def flip(axis, size, bits):
+    return [(place, place ^ bits) for place in range(size)]
+
+
+def gather_rows(block, axis, size):
+    kept = [block] + [
+        lax.ppermute(block, axis, flip(axis, size, bits)) for bits in range(2, size, 2)
+    ]
+    same_core = jnp.concatenate(kept, axis=0)
+    other_core = lax.ppermute(same_core, axis, flip(axis, size, 1))
+    return same_core, other_core
+
+
+def scatter_rows(same_core, other_core, axis, size):
+    arrived = lax.ppermute(other_core.astype(jnp.bfloat16), axis, flip(axis, size, 1))
+    rows = same_core.shape[0] // (size // 2)
+    pair = same_core + arrived.astype(jnp.float32)
+    own = pair[:rows]
+    sent = pair[rows:].astype(jnp.bfloat16)
+    for place, bits in enumerate(range(2, size, 2)):
+        piece = lax.ppermute(
+            sent[place * rows : (place + 1) * rows], axis, flip(axis, size, bits)
+        )
+        own = own + piece.astype(jnp.float32)
+    return own
+
+
+def dot_nt(left, right):
+    return lax.dot_general(
+        left, right, (((1,), (1,)), ((), ())), preferred_element_type=jnp.float32
+    )
+
+
+def dot_tn(left, right):
+    return lax.dot_general(
+        left, right, (((0,), (0,)), ((), ())), preferred_element_type=jnp.float32
+    )
+
+
+def dot_nn(left, right):
+    return jnp.dot(left, right, preferred_element_type=jnp.float32)
+
+
+def build_split(dp_size, zero_size):
+    copies = zero_size // KEY_VALUE_HEADS
+    per_dp = KEY_VALUE_HEADS // dp_size if KEY_VALUE_HEADS % dp_size == 0 else 0
+    regroup = copies == 1 and per_dp > 0
+    local_heads = QUERY_HEADS // zero_size
+    query_width = local_heads * HEAD_SIZE
+    local_width = query_width + 2 * HEAD_SIZE
+    query_span = QUERY_HEADS * HEAD_SIZE
+    key_span = KEY_VALUE_HEADS * HEAD_SIZE
+    score_scale = HEAD_SIZE ** (-0.5)
+    places = [place for place in range(0, zero_size, 2)] + [
+        place for place in range(1, zero_size, 2)
+    ]
+
+    def spread_heads(rows, width):
+        count = rows.shape[0]
+        if regroup:
+            parts = rows.reshape(count, dp_size, per_dp, width)
+            return jnp.transpose(parts, (2, 1, 0, 3)).reshape(zero_size, count, width)
+        return jnp.transpose(rows.reshape(count, zero_size, width), (1, 0, 2))
+
+    def join_heads(parts):
+        count, width = parts.shape[1:]
+        if regroup:
+            split = parts.reshape(per_dp, dp_size, count, width)
+            return jnp.transpose(split, (2, 1, 0, 3)).reshape(count, zero_size * width)
+        return jnp.transpose(parts, (1, 0, 2)).reshape(count, zero_size * width)
+
+    def spread_qkv(rows):
+        query = spread_heads(rows[:, :query_span], query_width)
+        key = rows[:, query_span : query_span + key_span]
+        value = rows[:, query_span + key_span :]
+        if copies > 1:
+            key, value = [
+                jnp.repeat(part.reshape(-1, KEY_VALUE_HEADS, HEAD_SIZE), copies, axis=1).reshape(
+                    rows.shape[0], -1
+                )
+                for part in (key, value)
+            ]
+        return jnp.concatenate(
+            [query, spread_heads(key, HEAD_SIZE), spread_heads(value, HEAD_SIZE)], axis=-1
+        )
+
+    def join_qkv(parts):
+        query = join_heads(parts[..., :query_width])
+        key, value = [
+            join_heads(parts[..., start : start + HEAD_SIZE])
+            for start in (query_width, query_width + HEAD_SIZE)
+        ]
+        if copies > 1:
+            key, value = [
+                part.reshape(-1, KEY_VALUE_HEADS, copies, HEAD_SIZE)
+                .sum(axis=2)
+                .reshape(query.shape[0], key_span)
+                for part in (key, value)
+            ]
+        return jnp.concatenate([query, key, value], axis=-1)
+
+    def spread_units(rows):
+        count = rows.shape[0]
+        units = FF // (dp_size * zero_size)
+        parts = rows.reshape(count, 2, dp_size, zero_size, units)
+        return jnp.transpose(parts, (3, 0, 1, 2, 4)).reshape(zero_size, count, 2 * FF // zero_size)
+
+    def join_units(parts):
+        count = parts.shape[1]
+        units = FF // (dp_size * zero_size)
+        split = parts.reshape(zero_size, count, 2, dp_size, units)
+        return jnp.transpose(split, (1, 2, 3, 0, 4)).reshape(count, 2 * FF)
+
+    groups = None
+    if regroup:
+        groups = [
+            [part * dp_size + place for place in range(dp_size)] for part in range(per_dp)
+        ]
+
+    def gather_out(rows):
+        if regroup:
+            by_dp = lax.all_gather(rows, "dp", axis=0, tiled=False)
+            mine = lax.all_to_all(by_dp, "zero", 0, 0, axis_index_groups=groups, tiled=True)
+            return mine.reshape(query_width, rows.shape[1])
+        every = lax.all_gather(rows, ("dp", "zero"), axis=0, tiled=True)
+        return lax.dynamic_slice_in_dim(every, lax.axis_index("zero") * query_width, query_width)
+
+    def scatter_out(grad):
+        if regroup:
+            parts = grad.reshape(dp_size, query_width // dp_size, grad.shape[1])
+            by_dp = lax.all_to_all(parts, "zero", 0, 0, axis_index_groups=groups, tiled=True)
+            return lax.psum_scatter(by_dp, "dp", scatter_dimension=0, tiled=False)
+        every = jnp.zeros((query_span, grad.shape[1]), grad.dtype)
+        every = lax.dynamic_update_slice_in_dim(
+            every, grad, lax.axis_index("zero") * query_width, 0
+        )
+        return lax.psum_scatter(every, ("dp", "zero"), scatter_dimension=0, tiled=True)
+
+    def on_device_split(
+        block_input,
+        out_cotangent,
+        segment_ids,
+        query_key_value_weight,
+        w_out,
+        w_gateup,
+        w_down,
+        norm_gains,
+        head_gains,
+        first_moment_projection,
+        mean_out,
+        mean_gateup,
+        mean_down,
+        mean_norms,
+        mean_heads,
+        second_moment_projection,
+        square_out,
+        square_gateup,
+        square_down,
+        square_norms,
+        square_heads,
+    ):
+        masters = (query_key_value_weight, w_out, w_gateup, w_down, norm_gains, head_gains)
+        means = (first_moment_projection, mean_out, mean_gateup, mean_down, mean_norms, mean_heads)
+        squares = (
+            second_moment_projection,
+            square_out,
+            square_gateup,
+            square_down,
+            square_norms,
+            square_heads,
+        )
+        inputs = block_input[0]
+        cotangent = out_cotangent[0]
+        segments = segment_ids[0]
+        token_rows = inputs.shape[0]
+        sequence_length = segments.shape[0]
+        half_length = sequence_length // 2
+        width = inputs.shape[1]
+        weight_rows = query_key_value_weight.shape[0]
+        head_rows = head_gains.shape[0]
+        low = lambda value: value.astype(jnp.bfloat16)
+        wide = lambda value: value.astype(jnp.float32)
+        place = lax.axis_index("zero")
+
+        gains = wide(low(norm_gains))
+        low_qkv = wide(low(query_key_value_weight))
+        low_gateup = wide(low(w_gateup))
+        scaled_qkv = low(low_qkv * gains[:, 0:1])
+        scaled_gateup = low(low_gateup * gains[:, 1:2])
+        small = jnp.zeros((weight_rows, HEAD_SIZE), jnp.bfloat16)
+        small = lax.dynamic_update_slice(small, low(head_gains), (0, 0))
+        small = jnp.broadcast_to(small[None], (zero_size, weight_rows, HEAD_SIZE))
+        outgoing = jnp.concatenate(
+            [spread_qkv(scaled_qkv), spread_units(scaled_gateup), small], axis=-1
+        )
+        incoming = lax.all_to_all(outgoing, "zero", 0, 0, tiled=True)
+        group_rows = zero_size * weight_rows
+        head_part = incoming[:, :head_rows, local_width + 2 * FF // zero_size :][..., :2]
+        head_part = head_part.reshape(1, zero_size * head_rows * 2)
+        head_part = jnp.pad(head_part, ((0, 15), (0, local_width - head_part.shape[1])))
+        qkv_part = incoming[..., :local_width].reshape(group_rows, local_width)
+        gateup_part = incoming[..., local_width : local_width + 2 * FF // zero_size].reshape(
+            group_rows, 2 * FF // zero_size
+        )
+        qkv_every = lax.all_gather(
+            jnp.concatenate([qkv_part, head_part], axis=0), "dp", axis=0, tiled=False
+        )
+        qkv_weight = qkv_every[:, :group_rows].reshape(width, local_width)
+        heads = qkv_every[:, group_rows, : zero_size * head_rows * 2].reshape(HEAD_SIZE, 2)
+        out_weight = gather_out(low(w_out))
+        gateup_weight = lax.all_gather(gateup_part, "dp", axis=0, tiled=True)
+        down_weight = lax.all_gather(low(w_down), "dp", axis=0, tiled=True)
+        query_gain = wide(heads[:, 0])
+        key_gain = wide(heads[:, 1])
+
+        scale_one = rms_scale(inputs)
+        unit_one = inputs * scale_one
+        one_same, one_other = gather_rows(low(unit_one), "zero", zero_size)
+        unit_full = jnp.concatenate([one_same, one_other], axis=0)
+        cot_same, cot_other = gather_rows(low(cotangent), "zero", zero_size)
+        cot_full = jnp.concatenate([cot_same, cot_other], axis=0)
+
+        blocks = jnp.bitwise_xor(place, jnp.array(places, jnp.int32))
+        positions = (
+            blocks[:, None] * token_rows + jnp.arange(token_rows, dtype=jnp.int32)[None, :]
+        ).reshape(sequence_length)
+        ordered = jnp.take(segments.reshape(zero_size, token_rows), blocks, axis=0).reshape(
+            sequence_length
+        )
+        cosine, sine = rope_tables(positions, HEAD_SIZE)
+        allowed = (ordered[:, None] == ordered[None, :]) & (
+            positions[:, None] >= positions[None, :]
+        )
+
+        projected = dot_nn(unit_full, qkv_weight)
+        query = projected[:, :query_width].reshape(sequence_length, local_heads, HEAD_SIZE)
+        key = projected[:, query_width : query_width + HEAD_SIZE]
+        value_low = low(projected[:, query_width + HEAD_SIZE :])
+        query_scale = rms_scale(query)
+        key_scale = rms_scale(key)
+        query_normed = query * query_scale * query_gain
+        key_normed = key * key_scale * key_gain
+        query_turned = low(
+            query_normed * cosine[:, None, :] + rotate_half(query_normed) * sine[:, None, :]
+        )
+        key_turned = low(key_normed * cosine + rotate_half(key_normed) * sine)
+
+        softs, lows, outs = [], [], []
+        for head in range(local_heads):
+            scores = dot_nt(query_turned[:, head], key_turned) * score_scale
+            scores = jnp.where(allowed, scores, score_masked)
+            top = jnp.max(scores, axis=-1, keepdims=True)
+            weights = jnp.where(allowed, jnp.exp(scores - top), 0.0)
+            soft = weights / jnp.sum(weights, axis=-1, keepdims=True)
+            soft_low = low(soft)
+            softs.append(soft)
+            lows.append(soft_low)
+            outs.append(low(dot_nn(soft_low, value_low)))
+        attended = jnp.concatenate(outs, axis=-1)
+
+        attended_same, attended_other = attended[:half_length], attended[half_length:]
+        middle = inputs + scatter_rows(
+            dot_nn(attended_same, out_weight), dot_nn(attended_other, out_weight), "zero", zero_size
+        )
+        scale_two = rms_scale(middle)
+        unit_two = middle * scale_two
+        two_same, two_other = gather_rows(low(unit_two), "zero", zero_size)
+        two_full = jnp.concatenate([two_same, two_other], axis=0)
+        gateup = dot_nn(two_full, gateup_weight)
+        units = FF // zero_size
+        gate = gateup[:, :units]
+        upward = gateup[:, units:]
+        sigma = jax.nn.sigmoid(gate)
+        hidden = low(gate * sigma * upward)
+        output = middle + scatter_rows(
+            dot_nn(hidden[:half_length], down_weight),
+            dot_nn(hidden[half_length:], down_weight),
+            "zero",
+            zero_size,
+        )
+        grad_hidden = dot_nt(cot_full, down_weight)
+        gate_term = grad_hidden * upward * sigma * (1.0 + gate * (1.0 - sigma))
+        up_term = grad_hidden * gate * sigma
+        gateup_grad = low(jnp.concatenate([gate_term, up_term], axis=-1))
+        scaled_grad = scatter_rows(
+            dot_nt(gateup_grad[:half_length], gateup_weight),
+            dot_nt(gateup_grad[half_length:], gateup_weight),
+            "zero",
+            zero_size,
+        )
+        down_sum = lax.psum_scatter(
+            low(dot_tn(hidden, cot_full)), "dp", scatter_dimension=0, tiled=True
+        )
+        gateup_sum = lax.psum_scatter(
+            low(dot_tn(two_full, gateup_grad)), "dp", scatter_dimension=0, tiled=True
+        )
+        grad_middle = cotangent + rms_back(scaled_grad, middle, scale_two)
+        low_same, low_other = gather_rows(low(grad_middle), "zero", zero_size)
+        middle_low = jnp.concatenate([low_same, low_other], axis=0)
+        attended_grad = low(dot_nt(middle_low, out_weight))
+        out_sum = scatter_out(low(dot_tn(attended, middle_low)))
+
+        query_grads = []
+        key_grad = jnp.zeros((sequence_length, HEAD_SIZE), jnp.float32)
+        value_grad = jnp.zeros((sequence_length, HEAD_SIZE), jnp.float32)
+        for head in range(local_heads):
+            span = slice(head * HEAD_SIZE, (head + 1) * HEAD_SIZE)
+            grad_out_head = attended_grad[:, span]
+            delta = jnp.sum(wide(grad_out_head) * wide(outs[head]), axis=-1, keepdims=True)
+            grad_soft = dot_nt(grad_out_head, value_low)
+            grad_scores = low(softs[head] * (grad_soft - delta))
+            query_grads.append(dot_nn(grad_scores, key_turned) * score_scale)
+            key_grad = key_grad + dot_tn(grad_scores, query_turned[:, head]) * score_scale
+            value_grad = value_grad + dot_tn(lows[head], grad_out_head)
+        grad_query = jnp.stack(query_grads, axis=1)
+        query_back = grad_query * cosine[:, None, :] + rotate_back(grad_query * sine[:, None, :])
+        key_back = key_grad * cosine + rotate_back(key_grad * sine)
+        gain_query = jnp.sum(query_back * query * query_scale, axis=(0, 1))
+        gain_key = jnp.sum(key_back * key * key_scale, axis=0)
+        query_pre = rms_back(query_back * query_gain, query, query_scale)
+        key_pre = rms_back(key_back * key_gain, key, key_scale)
+        grad_projected = low(
+            jnp.concatenate(
+                [query_pre.reshape(sequence_length, query_width), key_pre, value_grad], axis=-1
+            )
+        )
+        qkv_partial = low(dot_tn(unit_full, grad_projected)).reshape(
+            dp_size, group_rows, local_width
+        )
+        head_partial = low(jnp.stack([gain_query, gain_key], axis=1)).reshape(dp_size, 1, -1)
+        head_partial = jnp.pad(
+            head_partial, ((0, 0), (0, 15), (0, local_width - head_partial.shape[2]))
+        )
+        qkv_sum = lax.psum_scatter(
+            jnp.concatenate([qkv_partial, head_partial], axis=1),
+            "dp",
+            scatter_dimension=0,
+            tiled=False,
+        )
+        input_part = scatter_rows(
+            dot_nt(grad_projected[:half_length], qkv_weight),
+            dot_nt(grad_projected[half_length:], qkv_weight),
+            "zero",
+            zero_size,
+        )
+        grad_input = grad_middle + rms_back(input_part, inputs, scale_one)
+
+        head_back = qkv_sum[group_rows, : zero_size * head_rows * 2].reshape(
+            zero_size, head_rows, 2
+        )
+        head_back = jnp.pad(
+            head_back, ((0, 0), (0, weight_rows - head_rows), (0, HEAD_SIZE - 2))
+        )
+        returned = lax.all_to_all(
+            jnp.concatenate(
+                [
+                    qkv_sum[:group_rows].reshape(zero_size, weight_rows, local_width),
+                    gateup_sum.reshape(zero_size, weight_rows, 2 * FF // zero_size),
+                    head_back,
+                ],
+                axis=-1,
+            ),
+            "zero",
+            0,
+            0,
+            tiled=True,
+        )
+        bare_qkv = join_qkv(wide(returned[..., :local_width]))
+        bare_gateup = join_units(
+            wide(returned[..., local_width : local_width + 2 * FF // zero_size])
+        )
+        grad_heads = jnp.sum(
+            wide(returned[:, :head_rows, local_width + 2 * FF // zero_size :][..., :2]), axis=0
+        )
+        grad_norms = jnp.stack(
+            [row_sum(low_qkv * bare_qkv), row_sum(low_gateup * bare_gateup)], axis=1
+        )
+        summed = (
+            bare_qkv * gains[:, 0:1],
+            wide(out_sum),
+            bare_gateup * gains[:, 1:2],
+            wide(down_sum),
+            grad_norms,
+            grad_heads,
+        )
+        updated = [
+            adam_update(masters[index], summed[index], means[index], squares[index])
+            for index in range(6)
+        ]
+        return (
+            output[None],
+            grad_input[None],
+            *summed,
+            *[update[0] for update in updated],
+            *[update[1] for update in updated],
+            *[update[2] for update in updated],
+        )
+
+    return on_device_split
+
+
+def can_split(dp_size, zero_size):
+    return (
+        zero_size >= 2
+        and zero_size & (zero_size - 1) == 0
+        and zero_size % KEY_VALUE_HEADS == 0
+        and QUERY_HEADS % zero_size == 0
+        and FF % (dp_size * zero_size) == 0
+    )
+
 
 def solution(mesh):
     placed = (
@@ -411,8 +825,10 @@
         P(("dp", "zero"), None),
         P(("dp", "zero"), None),
     )
+    sizes = (mesh.shape["dp"], mesh.shape["zero"])
+    body = build_split(*sizes) if can_split(*sizes) else on_device_gathered
     return jax.shard_map(
-        on_device,
+        body,
         mesh=mesh,
         in_specs=placed,
         out_specs=(

time: 1430 us -> 368 us (0.26)
  waiting for transfers between devices: 1100 us -> 130 us
  blocking collectives: 120 us -> 35.4 us
  starting transfers between devices: 1.3 us -> 46 us
  matrix products: 87 us -> 46.4 us
    reduce_scatter x6 -> x4, waiting for transfers between devices: 801 us -> 39.5 us  [the longest x1 24 us: on_device_split(): lax.psum_scatter(low(dot_tn(two_full, gateup_grad)), 'dp', scatter_dimens...]
    all_gather x6 -> x2, waiting for transfers between devices: 243 us -> 25.7 us  [the longest x1 25.7 us: on_device_split(): lax.all_gather(jnp.concatenate([qkv_part, head_part], axis=0), 'dp', axis...]
    ppermute x0 -> x32, waiting for transfers between devices: none -> 64.8 us  [the longest x12 44.3 us: scatter_rows(): lax.ppermute(sent[place * rows:(place + 1) * rows], axis, flip(axis, size...]
    unnamed x14 -> x6, waiting for transfers between devices: 54.2 us -> 0.1 us
    all_gather x2, blocking collectives: 80.9 us -> 35.4 us  [the longest x1 19 us: on_device_split(): down_weight = lax.all_gather(low(w_down), 'dp', axis=0, tiled=True)]
    unnamed x1 -> x0, blocking collectives: 39.4 us -> none
    dot_general x18 -> x28, matrix products: 83.9 us -> 46.4 us  [the longest x8 18.1 us: dot_tn(): lax.dot_general(left, right, (((0,), (0,)), ((), ())), preferred_element_...]
    ppermute x0 -> x32, starting transfers between devices: none -> 29.2 us  [the longest x12 14.9 us: gather_rows(): lax.ppermute(block, axis, flip(axis, size, bits))]
  transfers between devices with their start and end apart: 13 -> 42, of which waited for: 12 -> 21; matrix products, arithmetic and copies ran while one was open for 8% -> 26% of each run, Pallas kernels for 0% -> 0%
where the time goes in v1:
time: 368 us; the launch traced here: 364 us
  waiting for transfers between devices  130 us (35%)
  matrix products  46.4 us (13%)
  local copies, waits for them, and re-layouts  46 us (12%)
  starting transfers between devices  46 us (12%)
  other arithmetic  44.9 us (12%)
  blocking collectives  35.4 us (10%)
  between operations  15.7 us (4%)
    ppermute x12, waiting for transfers between devices, scatter_rows(): lax.ppermute(sent[place * rows:(place + 1) * rows], axis, flip(axis, size...  44.3 us
    unnamed x174, local copies, waits for them, and re-layouts  26.6 us
    all_gather x1, waiting for transfers between devices, on_device_split(): lax.all_gather(jnp.concatenate([qkv_part, head_part], axis=0), 'dp', axis...  25.7 us
    reduce_scatter x1, waiting for transfers between devices, on_device_split(): lax.psum_scatter(low(dot_tn(two_full, gateup_grad)), 'dp', scatter_dimens...  24 us
    all_gather x1, blocking collectives, on_device_split(): down_weight = lax.all_gather(low(w_down), 'dp', axis=0, tiled=True)  19 us
    dot_general x8, matrix products, dot_tn(): lax.dot_general(left, right, (((0,), (0,)), ((), ())), preferred_element_...  18.1 us
    ppermute x12, waiting for transfers between devices, gather_rows(): lax.ppermute(block, axis, flip(axis, size, bits))  17.4 us
    all_gather x1, blocking collectives, gather_out(): by_dp = lax.all_gather(rows, 'dp', axis=0, tiled=False)  16.4 us
  transfers between devices with their start and end apart: 42, of which 21 were waited for; matrix products, arithmetic and copies ran while one was open for 26% of the time, Pallas kernels for 0%

profile of v1, /device:TPU:0, one launch (start us, length us, event | category | flops | bytes accessed | tf_op | source)
XLA Modules:
  0.0 364.5 jit_solution(17572897786296417111)
XLA Ops:
  15.4 5.2 %all-to-all-start = ((bf16[8,32,1408]{2,1,0:T(8,128)(2,1)}), bf16[8,32,1408]{2,1,0:T(8,128)(2,1)S(1)}, u32[]{:S(2)}, u32[]{:S(2)}) async-start(bf16[8,32,1408]{2,1,0:T(8,128)(2,1)} %constant_dynamic-update-slice_fusion.5), calls=%async_computation | async-start | bytes 1441792 | tf_op jit(solution)/shard_map/all_to_all | solution.py:588
  21.6 2.9 collective-permute-start.2
  25.1 16.4 %all-gather.1 = bf16[256,1024]{1,0:T(8,128)(2,1)} all-gather(bf16[64,1024]{1,0:T(8,128)(2,1)S(1)} %convert_element_type.247), channel_id=3, replica_groups=mesh['dp'=4,'zero'=8] {'dp'}, dimensions={0}, use_global_device_ids=true | all-gather | bytes 655360 | tf_op jit(solution)/shard_map/all_gather | solution.py:514
  41.5 3.5 all-to-all-start.1
  48.6 1.7 constant_dynamic-update-slice_fusion.3
  51.8 2.3 constant_dynamic-update-slice_fusion
  54.1 25.7 %all-gather.7.cloned.1.call-done = bf16[1088,512]{1,0:T(8,128)(2,1)} async-done(((bf16[272,512]{1,0:T(8,128)(2,1)}), bf16[1088,512]{1,0:T(8,128)(2,1)}) %all-gather.7.cloned.1.call-update) | async-done | bytes 1114128 | tf_op jit(solution)/shard_map/all_gather | solution.py:597
  84.3 2.2 fusion.57
  87.8 1.6 fusion.1
  89.4 2.9 fusion.5
  92.3 3.2 fusion.4
  95.5 1.5 convolution_convert_fusion.9
  100.1 1.6 convolution_convert_fusion.4
  101.9 2.6 collective-permute-done.4
  104.5 1.9 fusion.111
  107.3 1.5 collective-permute-start.5
  108.8 1.5 collective-permute-start.7
  111.7 2.4 collective-permute-start.18
  116.7 1.5 collective-permute-start.16
  118.2 5.2 %collective-permute-done.7 = bf16[128,1024]{1,0:T(8,128)(2,1)S(1)} collective-permute-done((bf16[128,1024]{1,0:T(8,128)(2,1)}, bf16[128,1024]{1,0:T(8,128)(2,1)S(1)}, u32[]{:S(2)}, u32[]{:S(2)}) %collective-permute-start.7) | collective-permute-done | bytes 262176 | tf_op jit(solution)/shard_map/ppermute | solution.py:413
  123.3 7.7 %collective-permute-done.6 = bf16[128,1024]{1,0:T(8,128)(2,1)} collective-permute-done((bf16[128,1024]{1,0:T(8,128)(2,1)}, bf16[128,1024]{1,0:T(8,128)(2,1)}, u32[]{:S(2)}, u32[]{:S(2)}) %collective-permute-start.6) | collective-permute-done | bytes 262176 | tf_op jit(solution)/shard_map/ppermute | solution.py:413
  131.0 1.5 multiply_reduce_fusion.8
  133.4 1.4 collective-permute-start.10
  134.8 1.5 collective-permute-start.9
  136.9 4.0 %collective-permute-done.17 = bf16[128,1024]{1,0:T(8,128)(2,1)} collective-permute-done((bf16[128,1024]{1,0:T(8,128)(2,1)}, bf16[128,1024]{1,0:T(8,128)(2,1)}, u32[]{:S(2)}, u32[]{:S(2)}) %collective-permute-start.17) | collective-permute-done | bytes 262176 | tf_op jit(solution)/shard_map/ppermute | solution.py:399
  142.3 4.1 %collective-permute-done.9 = bf16[128,1024]{1,0:T(8,128)(2,1)S(1)} collective-permute-done((bf16[128,1024]{1,0:T(8,128)(2,1)S(1)}, bf16[128,1024]{1,0:T(8,128)(2,1)S(1)}, u32[]{:S(2)}, u32[]{:S(2)}) %collective-permute-start.9) | collective-permute-done | bytes 262176 | tf_op jit(solution)/shard_map/ppermute | solution.py:399
  146.5 19.0 %all_gather.23 = bf16[384,1024]{1,0:T(8,128)(2,1)} all-gather(bf16[96,1024]{1,0:T(8,128)(2,1)S(1)} %convert_element_type.255), channel_id=1, replica_groups=mesh['dp'=4,'zero'=8] {'dp'}, dimensions={0}, use_global_device_ids=true | all-gather | bytes 983040 | tf_op jit(solution)/shard_map/all_gather | solution.py:604
  170.9 4.1 %fusion.120 = f32[1024,768]{0,1:T(8,128)S(1)} fusion(bf16[1024,1024]{1,0:T(8,128)(2,1)} %constant_dynamic-update-slice_fusion.10, bf16[1024,768]{1,0:T(8,128)(2,1)} %all-gather.5.cloned.1.call-done), kind=kOutput, calls=%fused_computation.279 | convolution fusion | flops 1610612736 | bytes 6815744 | tf_op jit(solution)/shard_map/dot_general | solution.py:433
  175.0 1.6 multiply_convert_fusion.2
  180.9 1.5 collective-permute-start.13
  182.9 1.6 collective-permute-start.14
  185.6 1.5 collective-permute-start.21
  187.5 2.6 collective-permute-done.13
  190.6 5.1 %collective-permute-done.15 = bf16[128,1024]{1,0:T(8,128)(2,1)S(1)} collective-permute-done((bf16[128,1024]{1,0:T(8,128)(2,1)S(1)}, bf16[128,1024]{1,0:T(8,128)(2,1)S(1)}, u32[]{:S(2)}, u32[]{:S(2)}) %collective-permute-start.15) | collective-permute-done | bytes 262176 | tf_op jit(solution)/shard_map/ppermute | solution.py:413
  195.7 2.0 collective-permute-done.14
  197.6 3.8 %collective-permute-done.21 = bf16[128,1024]{1,0:T(8,128)(2,1)S(1)} collective-permute-done((bf16[128,1024]{1,0:T(8,128)(2,1)S(1)}, bf16[128,1024]{1,0:T(8,128)(2,1)S(1)}, u32[]{:S(2)}, u32[]{:S(2)}) %collective-permute-start.21) | collective-permute-done | bytes 262176 | tf_op jit(solution)/shard_map/ppermute | solution.py:413
  201.4 4.8 %collective-permute-done.23 = bf16[128,1024]{1,0:T(8,128)(2,1)S(1)} collective-permute-done((bf16[128,1024]{1,0:T(8,128)(2,1)S(1)}, bf16[128,1024]{1,0:T(8,128)(2,1)S(1)}, u32[]{:S(2)}, u32[]{:S(2)}) %collective-permute-start.23) | collective-permute-done | bytes 262176 | tf_op jit(solution)/shard_map/ppermute | solution.py:413
  209.7 2.5 collective-permute-start.26
  213.2 6.3 %collective-permute-done.26 = bf16[128,1024]{1,0:T(8,128)(2,1)S(1)} collective-permute-done((bf16[128,1024]{1,0:T(8,128)(2,1)S(1)}, bf16[128,1024]{1,0:T(8,128)(2,1)S(1)}, u32[]{:S(2)}, u32[]{:S(2)}) %collective-permute-start.26) | collective-permute-done | bytes 262176 | tf_op jit(solution)/shard_map/ppermute | solution.py:399
  219.6 2.8 collective-permute-done.25
  223.6 1.9 convolution_convert_fusion.6
  225.9 1.7 constant_dynamic-update-slice_fusion.23
  229.1 2.3 constant_dynamic-update-slice_fusion.20
  231.4 2.6 convolution_convert_fusion.8
  238.9 2.3 fusion.85
  241.3 2.6 multiply_reduce_fusion.2
  248.2 3.2 fusion.21
  256.5 4.6 %convolution_convert_fusion = bf16[1024,768]{1,0:T(8,128)(2,1)} fusion(bf16[1024,1024]{1,0:T(8,128)(2,1)} %constant_dynamic-update-slice_fusion.10, bf16[1024,384]{0,1:T(8,128)(2,1)S(1)} %copy-done.46, bf16[1024,384]{0,1:T(8,128)(2,1)S(1)} %copy-done.48), kind=kOutput, calls=%fused_computation.28 | convolution fusion | flops 1614544896 | bytes 5242880 | tf_op jit(solution)/shard_map/dot_general | solution.py:427
  262.3 1.8 convolution_convert_fusion.5
  264.9 3.1 convolution_convert_fusion.7
  268.1 3.5 all-to-all-start.3
  271.6 2.5 fusion.114
  275.0 1.9 collective-permute-start.29
  278.5 2.4 multiply_subtract_fusion.2
  281.8 4.8 %collective-permute-done.29 = bf16[128,1024]{1,0:T(8,128)(2,1)} collective-permute-done((bf16[128,1024]{1,0:T(8,128)(2,1)}, bf16[128,1024]{1,0:T(8,128)(2,1)}, u32[]{:S(2)}, u32[]{:S(2)}) %collective-permute-start.29) | collective-permute-done | bytes 262176 | tf_op jit(solution)/shard_map/ppermute | solution.py:413
  286.6 5.9 %collective-permute-done.31 = bf16[128,1024]{1,0:T(8,128)(2,1)} collective-permute-done((bf16[128,1024]{1,0:T(8,128)(2,1)}, bf16[128,1024]{1,0:T(8,128)(2,1)}, u32[]{:S(2)}, u32[]{:S(2)}) %collective-permute-start.31) | collective-permute-done | bytes 262176 | tf_op jit(solution)/shard_map/ppermute | solution.py:413
  295.7 24.0 %reduce-scatter.7.cloned.1.call-done = bf16[256,768]{1,0:T(8,128)(2,1)} async-done(((bf16[1024,768]{1,0:T(8,128)(2,1)}), bf16[256,768]{1,0:T(8,128)(2,1)}) %reduce-scatter.7.cloned.1.call-update) | async-done | bytes 393232 | tf_op jit(solution)/shard_map/reduce_scatter | solution.py:686
  319.6 1.9 fusion.35
  321.6 3.7 %all-to-all-start.2 = ((bf16[8,32,1408]{2,1,0:T(8,128)(2,1)}), bf16[8,32,1408]{2,1,0:T(8,128)(2,1)S(1)}, u32[]{:S(2)}, u32[]{:S(2)}) async-start(bf16[8,32,1408]{2,1,0:T(8,128)(2,1)} %fusion.35), calls=%async_computation.4 | async-start | bytes 1441792 | tf_op jit(solution)/shard_map/all_to_all | solution.py:746
  325.2 2.3 add_bitcast_fusion
  327.5 15.6 %reduce-scatter.9.cloned.1.call-done = bf16[1,64,1024]{2,1,0:T(8,128)(2,1)} async-done(((bf16[4,64,1024]{2,1,0:T(8,128)(2,1)}), bf16[1,64,1024]{2,1,0:T(8,128)(2,1)}) %reduce-scatter.9.cloned.1.call-update) | async-done | bytes 131088 | tf_op jit(solution)/shard_map/reduce_scatter | solution.py:524
  343.1 2.2 multiply_subtract_fusion.3
  352.3 1.7 multiply_subtract_fusion.1
  354.7 2.1 multiply_subtract_fusion
  (346 shorter events, 81.8 us)
Async XLA Ops:
  7.2 40.7 %copy-start = (s32[1,1024]{1,0:T(1,128)S(1)}, s32[1,1024]{1,0:T(1,128)}, u32[]{:S(2)}) copy-start(s32[1,1024]{1,0:T(1,128)} %param.24) | copy-start | bytes 12292
  11.6 9.0 %copy-start.7 = (f32[1,128,1024]{2,1,0:T(8,128)S(1)}, f32[1,128,1024]{2,1,0:T(8,128)}, u32[]{:S(2)}) copy-start(f32[1,128,1024]{2,1,0:T(8,128)} %param.22) | copy-start | bytes 1572868
  12.7 12.4 %copy-start.40 = (f32[64,1024]{1,0:T(8,128)S(1)}, f32[64,1024]{1,0:T(8,128)}, u32[]{:S(2)}) copy-start(f32[64,1024]{1,0:T(8,128)} %param.26) | copy-start | bytes 786436
  15.4 26.1 %all-to-all-start = ((bf16[8,32,1408]{2,1,0:T(8,128)(2,1)}), bf16[8,32,1408]{2,1,0:T(8,128)(2,1)S(1)}, u32[]{:S(2)}, u32[]{:S(2)}) async-start(bf16[8,32,1408]{2,1,0:T(8,128)(2,1)} %constant_dynamic-update-slice_fusion.5), calls=%async_computation | async-start | bytes 1441792 | tf_op jit(solution)/shard_map/all_to_all | solution.py:588
  20.7 25.4 %copy-start.73 = (s32[8]{0:T(128)S(1)}, s32[8]{0:T(128)}, u32[]{:S(2)}) copy-start(s32[8]{0:T(128)} %constant.56.clone) | copy-start | bytes 100
  21.6 24.7 %copy-start.44 = (bf16[128,1024]{1,0:T(8,128)(2,1)}, bf16[128,1024]{1,0:T(8,128)(2,1)S(1)}, u32[]{:S(2)}) copy-start(bf16[128,1024]{1,0:T(8,128)(2,1)S(1)} %get-tuple-element.126) | copy-start | bytes 786436
  21.6 24.6 %collective-permute-start.2 = (bf16[128,1024]{1,0:T(8,128)(2,1)S(1)}, bf16[128,1024]{1,0:T(8,128)(2,1)S(1)}, u32[]{:S(2)}, u32[]{:S(2)}) collective-permute-start(bf16[128,1024]{1,0:T(8,128)(2,1)S(1)} %get-tuple-element.126), channel_id=1, source_target_pairs={{0,6},{1,7},{2,4},{3,5},{4,2},{5,3},{6,0},{7,1},{8,14},{9,15},{10,... | collective-permute-start | bytes 786440 | tf_op jit(solution)/shard_map/ppermute | solution.py:399
  24.5 21.7 %collective-permute-start.1 = (bf16[128,1024]{1,0:T(8,128)(2,1)S(1)}, bf16[128,1024]{1,0:T(8,128)(2,1)S(1)}, u32[]{:S(2)}, u32[]{:S(2)}) collective-permute-start(bf16[128,1024]{1,0:T(8,128)(2,1)S(1)} %get-tuple-element.126), channel_id=1, source_target_pairs={{0,4},{1,5},{2,6},{3,7},{4,0},{5,1},{6,2},{7,3},{8,12},{9,13},{10,... | collective-permute-start | bytes 786440 | tf_op jit(solution)/shard_map/ppermute | solution.py:399
  25.1 21.2 %collective-permute-start = (bf16[128,1024]{1,0:T(8,128)(2,1)S(1)}, bf16[128,1024]{1,0:T(8,128)(2,1)}, u32[]{:S(2)}, u32[]{:S(2)}) collective-permute-start(bf16[128,1024]{1,0:T(8,128)(2,1)S(1)} %get-tuple-element.126), channel_id=1, source_target_pairs={{0,2},{1,3},{2,0},{3,1},{4,6},{5,7},{6,4},{7,5},{8,10},{9,11},{10,... | collective-permute-start | bytes 786440 | tf_op jit(solution)/shard_map/ppermute | solution.py:399
  41.5 5.9 %copy-start.28 = (bf16[8,32,1408]{2,1,0:T(8,128)(2,1)}, bf16[8,32,1408]{2,1,0:T(8,128)(2,1)S(1)}, u32[]{:S(2)}) copy-start(bf16[8,32,1408]{2,1,0:T(8,128)(2,1)S(1)} %all-to-all-done) | copy-start | bytes 2162692
  41.5 58.6 %all-to-all-start.1 = ((bf16[4,64,1024]{2,1,0:T(8,128)(2,1)}), bf16[4,64,1024]{2,1,0:T(8,128)(2,1)S(1)}, u32[]{:S(2)}, u32[]{:S(2)}) async-start(bf16[4,64,1024]{2,1,0:T(8,128)(2,1)} %bitcast.19), calls=%async_computation.1 | async-start | bytes 1048576 | tf_op jit(solution)/shard_map/all_to_all | solution.py:515
  45.0 34.8 %all-gather.7.cloned.1.call-start = ((), (), s32[]{:S(2)}) async-start(), calls=%async_computation.13 | async-start | bytes 1392640 | tf_op jit(solution)/shard_map/all_gather | solution.py:597
  46.0 124.9 %all-gather.5.cloned.1.call-start = ((), (), s32[]{:S(2)}) async-start(), calls=%async_computation.8 | async-start | bytes 1966080 | tf_op jit(solution)/shard_map/all_gather | solution.py:603
  47.4 4.3 %collective-permute-start.3 = (bf16[512,1024]{1,0:T(8,128)(2,1)S(1)}, bf16[512,1024]{1,0:T(8,128)(2,1)}, u32[]{:S(2)}, u32[]{:S(2)}) collective-permute-start(bf16[512,1024]{1,0:T(8,128)(2,1)S(1)} %pad_maximum_fusion.2), channel_id=1, source_target_pairs={{0,1},{1,0},{2,3},{3,2},{4,5},{5,4},{6,7},{7,6},{8,9},{9,8},{10,11... | collective-permute-start | bytes 3145736 | tf_op jit(solution)/shard_map/ppermute | solution.py:402
  100.1 6.3 %copy-start.8 = (bf16[4,64,1024]{2,1,0:T(8,128)(2,1)}, bf16[4,64,1024]{2,1,0:T(8,128)(2,1)S(1)}, u32[]{:S(2)}) copy-start(bf16[4,64,1024]{2,1,0:T(8,128)(2,1)S(1)} %all-to-all-done.1) | copy-start | bytes 1572868
  100.1 4.4 %copy-start.18 = (bf16[1024,128]{0,1:T(8,128)(2,1)S(1)}, bf16[1024,128]{0,1:T(8,128)(2,1)}, u32[]{:S(2)}) copy-start(bf16[1024,128]{0,1:T(8,128)(2,1)} %convolution_convert_fusion.10) | copy-start | bytes 786436
  101.8 9.0 %copy-start.31 = (f32[1,128,1024]{2,1,0:T(8,128)S(1)}, f32[1,128,1024]{2,1,0:T(8,128)}, u32[]{:S(2)}) copy-start(f32[1,128,1024]{2,1,0:T(8,128)} %param.23) | copy-start | bytes 1572868
  101.8 2.7 collective-permute-start.4
  106.4 8.2 %copy-start.29 = (bf16[8,32,1408]{2,1,0:T(8,128)(2,1)S(1)}, bf16[8,32,1408]{2,1,0:T(8,128)(2,1)}, u32[]{:S(2)}) copy-start(bf16[8,32,1408]{2,1,0:T(8,128)(2,1)} %copy-done.28) | copy-start | bytes 2162692
  107.3 9.4 %collective-permute-start.5 = (bf16[128,1024]{1,0:T(8,128)(2,1)}, bf16[128,1024]{1,0:T(8,128)(2,1)S(1)}, u32[]{:S(2)}, u32[]{:S(2)}) collective-permute-start(bf16[128,1024]{1,0:T(8,128)(2,1)} %get-tuple-element.145), channel_id=1, source_target_pairs={{0,2},{1,3},{2,0},{3,1},{4,6},{5,7},{6,4},{7,5},{8,10},{9,11},{10,... | collective-permute-start | bytes 786440 | tf_op jit(solution)/shard_map/ppermute | solution.py:413
  108.8 14.6 %collective-permute-start.7 = (bf16[128,1024]{1,0:T(8,128)(2,1)}, bf16[128,1024]{1,0:T(8,128)(2,1)S(1)}, u32[]{:S(2)}, u32[]{:S(2)}) collective-permute-start(bf16[128,1024]{1,0:T(8,128)(2,1)} %get-tuple-element.146), channel_id=1, source_target_pairs={{0,6},{1,7},{2,4},{3,5},{4,2},{5,3},{6,0},{7,1},{8,14},{9,15},{10,... | collective-permute-start | bytes 786440 | tf_op jit(solution)/shard_map/ppermute | solution.py:413
  110.3 20.7 %collective-permute-start.6 = (bf16[128,1024]{1,0:T(8,128)(2,1)}, bf16[128,1024]{1,0:T(8,128)(2,1)}, u32[]{:S(2)}, u32[]{:S(2)}) collective-permute-start(bf16[128,1024]{1,0:T(8,128)(2,1)} %get-tuple-element.147), channel_id=1, source_target_pairs={{0,4},{1,5},{2,6},{3,7},{4,0},{5,1},{6,2},{7,3},{8,12},{9,13},{10,... | collective-permute-start | bytes 786440 | tf_op jit(solution)/shard_map/ppermute | solution.py:413
  111.7 24.6 %collective-permute-start.18 = (bf16[128,1024]{1,0:T(8,128)(2,1)}, bf16[128,1024]{1,0:T(8,128)(2,1)}, u32[]{:S(2)}, u32[]{:S(2)}) collective-permute-start(bf16[128,1024]{1,0:T(8,128)(2,1)} %get-tuple-element.118), channel_id=1, source_target_pairs={{0,6},{1,7},{2,4},{3,5},{4,2},{5,3},{6,0},{7,1},{8,14},{9,15},{10,... | collective-permute-start | bytes 786440 | tf_op jit(solution)/shard_map/ppermute | solution.py:399
  114.0 26.8 %collective-permute-start.17 = (bf16[128,1024]{1,0:T(8,128)(2,1)}, bf16[128,1024]{1,0:T(8,128)(2,1)}, u32[]{:S(2)}, u32[]{:S(2)}) collective-permute-start(bf16[128,1024]{1,0:T(8,128)(2,1)} %get-tuple-element.118), channel_id=1, source_target_pairs={{0,4},{1,5},{2,6},{3,7},{4,0},{5,1},{6,2},{7,3},{8,12},{9,13},{10,... | collective-permute-start | bytes 786440 | tf_op jit(solution)/shard_map/ppermute | solution.py:399
  115.4 163.1 %reduce-scatter.11.cloned.1.call-start = ((), (), s32[]{:S(2)}) async-start(), calls=%async_computation.12 | async-start | bytes 983040 | tf_op jit(solution)/shard_map/reduce_scatter | solution.py:683
  116.7 14.3 %copy-start.54 = (bf16[128,1024]{1,0:T(8,128)(2,1)}, bf16[128,1024]{1,0:T(8,128)(2,1)S(1)}, u32[]{:S(2)}) copy-start(bf16[128,1024]{1,0:T(8,128)(2,1)S(1)} %collective-permute-done.5) | copy-start | bytes 786436
  116.7 24.2 %collective-permute-start.16 = (bf16[128,1024]{1,0:T(8,128)(2,1)}, bf16[128,1024]{1,0:T(8,128)(2,1)S(1)}, u32[]{:S(2)}, u32[]{:S(2)}) collective-permute-start(bf16[128,1024]{1,0:T(8,128)(2,1)} %get-tuple-element.118), channel_id=1, source_target_pairs={{0,2},{1,3},{2,0},{3,1},{4,6},{5,7},{6,4},{7,5},{8,10},{9,11},{10,... | collective-permute-start | bytes 786440 | tf_op jit(solution)/shard_map/ppermute | solution.py:399
  123.3 7.7 %copy-start.55 = (bf16[128,1024]{1,0:T(8,128)(2,1)}, bf16[128,1024]{1,0:T(8,128)(2,1)S(1)}, u32[]{:S(2)}) copy-start(bf16[128,1024]{1,0:T(8,128)(2,1)S(1)} %collective-permute-done.7) | copy-start | bytes 786436
  132.5 9.7 %copy-start.38 = (f32[96,1024]{1,0:T(8,128)S(1)}, f32[96,1024]{1,0:T(8,128)}, u32[]{:S(2)}) copy-start(f32[96,1024]{1,0:T(8,128)} %param.28) | copy-start | bytes 1179652
  133.4 8.9 %collective-permute-start.10 = (bf16[128,1024]{1,0:T(8,128)(2,1)S(1)}, bf16[128,1024]{1,0:T(8,128)(2,1)S(1)}, u32[]{:S(2)}, u32[]{:S(2)}) collective-permute-start(bf16[128,1024]{1,0:T(8,128)(2,1)S(1)} %get-tuple-element.120), channel_id=1, source_target_pairs={{0,6},{1,7},{2,4},{3,5},{4,2},{5,3},{6,0},{7,1},{8,14},{9,15},{10,... | collective-permute-start | bytes 786440 | tf_op jit(solution)/shard_map/ppermute | solution.py:399
  134.8 11.5 %collective-permute-start.9 = (bf16[128,1024]{1,0:T(8,128)(2,1)S(1)}, bf16[128,1024]{1,0:T(8,128)(2,1)S(1)}, u32[]{:S(2)}, u32[]{:S(2)}) collective-permute-start(bf16[128,1024]{1,0:T(8,128)(2,1)S(1)} %get-tuple-element.120), channel_id=1, source_target_pairs={{0,4},{1,5},{2,6},{3,7},{4,0},{5,1},{6,2},{7,3},{8,12},{9,13},{10,... | collective-permute-start | bytes 786440 | tf_op jit(solution)/shard_map/ppermute | solution.py:399
  136.3 10.1 %collective-permute-start.8 = (bf16[128,1024]{1,0:T(8,128)(2,1)S(1)}, bf16[128,1024]{1,0:T(8,128)(2,1)S(1)}, u32[]{:S(2)}, u32[]{:S(2)}) collective-permute-start(bf16[128,1024]{1,0:T(8,128)(2,1)S(1)} %get-tuple-element.120), channel_id=1, source_target_pairs={{0,2},{1,3},{2,0},{3,1},{4,6},{5,7},{6,4},{7,5},{8,10},{9,11},{10,... | collective-permute-start | bytes 786440 | tf_op jit(solution)/shard_map/ppermute | solution.py:399
  142.1 23.3 %copy-start.56 = (bf16[1024,1024]{1,0:T(8,128)(2,1)S(1)}, bf16[1024,1024]{1,0:T(8,128)(2,1)}, u32[]{:S(2)}) copy-start(bf16[1024,1024]{1,0:T(8,128)(2,1)} %get-tuple-element.117) | copy-start | bytes 6291460
  142.1 25.3 %collective-permute-start.19 = (bf16[512,1024]{1,0:T(8,128)(2,1)S(1)}, bf16[512,1024]{1,0:T(8,128)(2,1)S(1)}, u32[]{:S(2)}, u32[]{:S(2)}) collective-permute-start(bf16[512,1024]{1,0:T(8,128)(2,1)S(1)} %pad_maximum_fusion.4), channel_id=1, source_target_pairs={{0,1},{1,0},{2,3},{3,2},{4,5},{5,4},{6,7},{7,6},{8,9},{9,8},{10,11... | collective-permute-start | bytes 3145736 | tf_op jit(solution)/shard_map/ppermute | solution.py:402
  146.4 23.3 %collective-permute-start.11 = (bf16[512,1024]{1,0:T(8,128)(2,1)S(1)}, bf16[512,1024]{1,0:T(8,128)(2,1)S(1)}, u32[]{:S(2)}, u32[]{:S(2)}) collective-permute-start(bf16[512,1024]{1,0:T(8,128)(2,1)S(1)} %pad_maximum_fusion.3), channel_id=1, source_target_pairs={{0,1},{1,0},{2,3},{3,2},{4,5},{5,4},{6,7},{7,6},{8,9},{9,8},{10,11... | collective-permute-start | bytes 3145736 | tf_op jit(solution)/shard_map/ppermute | solution.py:402
  176.6 7.9 %copy-start.45 = (bf16[1024,384]{0,1:T(8,128)(2,1)}, bf16[1024,384]{0,1:T(8,128)(2,1)S(1)}, u32[]{:S(2)}) copy-start(bf16[1024,384]{0,1:T(8,128)(2,1)S(1)} %get-tuple-element.127) | copy-start | bytes 2359300
  176.6 7.9 %copy-start.47 = (bf16[1024,384]{0,1:T(8,128)(2,1)}, bf16[1024,384]{0,1:T(8,128)(2,1)S(1)}, u32[]{:S(2)}) copy-start(bf16[1024,384]{0,1:T(8,128)(2,1)S(1)} %get-tuple-element.128) | copy-start | bytes 2359300
  177.3 2.7 collective-permute-start.12
  179.6 4.8 %collective-permute-start.20 = (bf16[512,1024]{1,0:T(8,128)(2,1)S(1)}, bf16[512,1024]{1,0:T(8,128)(2,1)S(1)}, u32[]{:S(2)}, u32[]{:S(2)}) collective-permute-start(bf16[512,1024]{1,0:T(8,128)(2,1)S(1)} %convolution_convert_fusion.1), channel_id=1, source_target_pairs={{0,1},{1,0},{2,3},{3,2},{4,5},{5,4},{6,7},{7,6},{8,9},{9,8},{10,11... | collective-permute-start | bytes 3145736 | tf_op jit(solution)/shard_map/ppermute | solution.py:407
  180.9 9.2 %collective-permute-start.13 = (bf16[128,1024]{1,0:T(8,128)(2,1)S(1)}, bf16[128,1024]{1,0:T(8,128)(2,1)S(1)}, u32[]{:S(2)}, u32[]{:S(2)}) collective-permute-start(bf16[128,1024]{1,0:T(8,128)(2,1)S(1)} %get-tuple-element.142), channel_id=1, source_target_pairs={{0,2},{1,3},{2,0},{3,1},{4,6},{5,7},{6,4},{7,5},{8,10},{9,11},{10,... | collective-permute-start | bytes 786440 | tf_op jit(solution)/shard_map/ppermute | solution.py:413
  182.4 13.3 %collective-permute-start.15 = (bf16[128,1024]{1,0:T(8,128)(2,1)S(1)}, bf16[128,1024]{1,0:T(8,128)(2,1)S(1)}, u32[]{:S(2)}, u32[]{:S(2)}) collective-permute-start(bf16[128,1024]{1,0:T(8,128)(2,1)S(1)} %get-tuple-element.143), channel_id=1, source_target_pairs={{0,6},{1,7},{2,4},{3,5},{4,2},{5,3},{6,0},{7,1},{8,14},{9,15},{10,... | collective-permute-start | bytes 786440 | tf_op jit(solution)/shard_map/ppermute | solution.py:413
  182.9 14.8 %collective-permute-start.14 = (bf16[128,1024]{1,0:T(8,128)(2,1)S(1)}, bf16[128,1024]{1,0:T(8,128)(2,1)S(1)}, u32[]{:S(2)}, u32[]{:S(2)}) collective-permute-start(bf16[128,1024]{1,0:T(8,128)(2,1)S(1)} %get-tuple-element.144), channel_id=1, source_target_pairs={{0,4},{1,5},{2,6},{3,7},{4,0},{5,1},{6,2},{7,3},{8,12},{9,13},{10,... | collective-permute-start | bytes 786440 | tf_op jit(solution)/shard_map/ppermute | solution.py:413
  185.5 23.1 %copy-start.32 = (f32[1,128,1024]{2,1,0:T(8,128)S(1)}, f32[1,128,1024]{2,1,0:T(8,128)}, u32[]{:S(2)}) copy-start(f32[1,128,1024]{2,1,0:T(8,128)} %param.23) | copy-start | bytes 1572868
  185.6 15.8 %collective-permute-start.21 = (bf16[128,1024]{1,0:T(8,128)(2,1)S(1)}, bf16[128,1024]{1,0:T(8,128)(2,1)S(1)}, u32[]{:S(2)}, u32[]{:S(2)}) collective-permute-start(bf16[128,1024]{1,0:T(8,128)(2,1)S(1)} %get-tuple-element.139), channel_id=1, source_target_pairs={{0,2},{1,3},{2,0},{3,1},{4,6},{5,7},{6,4},{7,5},{8,10},{9,11},{10,... | collective-permute-start | bytes 786440 | tf_op jit(solution)/shard_map/ppermute | solution.py:413
  187.1 19.1 %collective-permute-start.23 = (bf16[128,1024]{1,0:T(8,128)(2,1)S(1)}, bf16[128,1024]{1,0:T(8,128)(2,1)S(1)}, u32[]{:S(2)}, u32[]{:S(2)}) collective-permute-start(bf16[128,1024]{1,0:T(8,128)(2,1)S(1)} %get-tuple-element.140), channel_id=1, source_target_pairs={{0,6},{1,7},{2,4},{3,5},{4,2},{5,3},{6,0},{7,1},{8,14},{9,15},{10,... | collective-permute-start | bytes 786440 | tf_op jit(solution)/shard_map/ppermute | solution.py:413
  190.1 17.4 %collective-permute-start.22 = (bf16[128,1024]{1,0:T(8,128)(2,1)S(1)}, bf16[128,1024]{1,0:T(8,128)(2,1)S(1)}, u32[]{:S(2)}, u32[]{:S(2)}) collective-permute-start(bf16[128,1024]{1,0:T(8,128)(2,1)S(1)} %get-tuple-element.141), channel_id=1, source_target_pairs={{0,4},{1,5},{2,6},{3,7},{4,0},{5,1},{6,2},{7,3},{8,12},{9,13},{10,... | collective-permute-start | bytes 786440 | tf_op jit(solution)/shard_map/ppermute | solution.py:413
  209.7 9.8 %collective-permute-start.26 = (bf16[128,1024]{1,0:T(8,128)(2,1)S(1)}, bf16[128,1024]{1,0:T(8,128)(2,1)S(1)}, u32[]{:S(2)}, u32[]{:S(2)}) collective-permute-start(bf16[128,1024]{1,0:T(8,128)(2,1)S(1)} %get-tuple-element.115), channel_id=1, source_target_pairs={{0,6},{1,7},{2,4},{3,5},{4,2},{5,3},{6,0},{7,1},{8,14},{9,15},{10,... | collective-permute-start | bytes 786440 | tf_op jit(solution)/shard_map/ppermute | solution.py:399
  212.2 10.2 %collective-permute-start.25 = (bf16[128,1024]{1,0:T(8,128)(2,1)S(1)}, bf16[128,1024]{1,0:T(8,128)(2,1)S(1)}, u32[]{:S(2)}, u32[]{:S(2)}) collective-permute-start(bf16[128,1024]{1,0:T(8,128)(2,1)S(1)} %get-tuple-element.115), channel_id=1, source_target_pairs={{0,4},{1,5},{2,6},{3,7},{4,0},{5,1},{6,2},{7,3},{8,12},{9,13},{10,... | collective-permute-start | bytes 786440 | tf_op jit(solution)/shard_map/ppermute | solution.py:399
  212.7 9.9 %collective-permute-start.24 = (bf16[128,1024]{1,0:T(8,128)(2,1)S(1)}, bf16[128,1024]{1,0:T(8,128)(2,1)S(1)}, u32[]{:S(2)}, u32[]{:S(2)}) collective-permute-start(bf16[128,1024]{1,0:T(8,128)(2,1)S(1)} %get-tuple-element.115), channel_id=1, source_target_pairs={{0,2},{1,3},{2,0},{3,1},{4,6},{5,7},{6,4},{7,5},{8,10},{9,11},{10,... | collective-permute-start | bytes 786440 | tf_op jit(solution)/shard_map/ppermute | solution.py:399
  223.6 5.5 %collective-permute-start.27 = (bf16[512,1024]{1,0:T(8,128)(2,1)}, bf16[512,1024]{1,0:T(8,128)(2,1)}, u32[]{:S(2)}, u32[]{:S(2)}) collective-permute-start(bf16[512,1024]{1,0:T(8,128)(2,1)} %pad_maximum_fusion.5), channel_id=1, source_target_pairs={{0,1},{1,0},{2,3},{3,2},{4,5},{5,4},{6,7},{7,6},{8,9},{9,8},{10,11... | collective-permute-start | bytes 3145736 | tf_op jit(solution)/shard_map/ppermute | solution.py:402
  225.5 68.4 %reduce-scatter.5.cloned.1.call-start = ((), (), s32[]{:S(2)}) async-start(), calls=%async_computation.9 | async-start | bytes 1392640 | tf_op jit(solution)/shard_map/reduce_scatter | solution.py:726
  255.9 5.3 %copy-start.42 = (bf16[1024,128]{0,1:T(8,128)(2,1)S(1)}, bf16[1024,128]{0,1:T(8,128)(2,1)}, u32[]{:S(2)}) copy-start(bf16[1024,128]{0,1:T(8,128)(2,1)} %copy-done.41) | copy-start | bytes 786436
  255.9 63.8 %reduce-scatter.7.cloned.1.call-start = ((), (), s32[]{:S(2)}) async-start(), calls=%async_computation.10 | async-start | bytes 1966080 | tf_op jit(solution)/shard_map/reduce_scatter | solution.py:686
  264.1 7.5 %collective-permute-start.28 = (bf16[512,1024]{1,0:T(8,128)(2,1)}, bf16[512,1024]{1,0:T(8,128)(2,1)}, u32[]{:S(2)}, u32[]{:S(2)}) collective-permute-start(bf16[512,1024]{1,0:T(8,128)(2,1)} %convolution_convert_fusion.5), channel_id=1, source_target_pairs={{0,1},{1,0},{2,3},{3,2},{4,5},{5,4},{6,7},{7,6},{8,9},{9,8},{10,11... | collective-permute-start | bytes 3145736 | tf_op jit(solution)/shard_map/ppermute | solution.py:407
  268.1 12.9 %all-to-all-start.3 = ((bf16[4,64,1024]{2,1,0:T(8,128)(2,1)}), bf16[4,64,1024]{2,1,0:T(8,128)(2,1)S(1)}, u32[]{:S(2)}, u32[]{:S(2)}) async-start(bf16[4,64,1024]{2,1,0:T(8,128)(2,1)} %bitcast.44), calls=%async_computation.5 | async-start | bytes 1048576 | tf_op jit(solution)/shard_map/all_to_all | solution.py:523
  271.5 7.0 %copy-start.39 = (f32[96,1024]{1,0:T(8,128)S(1)}, f32[96,1024]{1,0:T(8,128)}, u32[]{:S(2)}) copy-start(f32[96,1024]{1,0:T(8,128)} %param.28) | copy-start | bytes 1179652
  271.5 71.6 %reduce-scatter.9.cloned.1.call-start = ((), (), s32[]{:S(2)}) async-start(), calls=%async_computation.11 | async-start | bytes 655360 | tf_op jit(solution)/shard_map/reduce_scatter | solution.py:524
  275.0 17.5 %copy-start.64 = (f32[128]{0:T(128)S(1)}, f32[128]{0:T(128)}, u32[]{:S(2)}) copy-start(f32[128]{0:T(128)} %copy-done.63) | copy-start | bytes 1540
  275.0 11.6 %collective-permute-start.29 = (bf16[128,1024]{1,0:T(8,128)(2,1)}, bf16[128,1024]{1,0:T(8,128)(2,1)}, u32[]{:S(2)}, u32[]{:S(2)}) collective-permute-start(bf16[128,1024]{1,0:T(8,128)(2,1)} %get-tuple-element.134), channel_id=1, source_target_pairs={{0,2},{1,3},{2,0},{3,1},{4,6},{5,7},{6,4},{7,5},{8,10},{9,11},{10,... | collective-permute-start | bytes 786440 | tf_op jit(solution)/shard_map/ppermute | solution.py:413
  277.0 15.5 %collective-permute-start.31 = (bf16[128,1024]{1,0:T(8,128)(2,1)}, bf16[128,1024]{1,0:T(8,128)(2,1)}, u32[]{:S(2)}, u32[]{:S(2)}) collective-permute-start(bf16[128,1024]{1,0:T(8,128)(2,1)} %get-tuple-element.135), channel_id=1, source_target_pairs={{0,6},{1,7},{2,4},{3,5},{4,2},{5,3},{6,0},{7,1},{8,14},{9,15},{10,... | collective-permute-start | bytes 786440 | tf_op jit(solution)/shard_map/ppermute | solution.py:413
  277.9 14.6 %collective-permute-start.30 = (bf16[128,1024]{1,0:T(8,128)(2,1)}, bf16[128,1024]{1,0:T(8,128)(2,1)}, u32[]{:S(2)}, u32[]{:S(2)}) collective-permute-start(bf16[128,1024]{1,0:T(8,128)(2,1)} %get-tuple-element.136), channel_id=1, source_target_pairs={{0,4},{1,5},{2,6},{3,7},{4,0},{5,1},{6,2},{7,3},{8,12},{9,13},{10,... | collective-permute-start | bytes 786440 | tf_op jit(solution)/shard_map/ppermute | solution.py:413
  321.6 23.7 %all-to-all-start.2 = ((bf16[8,32,1408]{2,1,0:T(8,128)(2,1)}), bf16[8,32,1408]{2,1,0:T(8,128)(2,1)S(1)}, u32[]{:S(2)}, u32[]{:S(2)}) async-start(bf16[8,32,1408]{2,1,0:T(8,128)(2,1)} %fusion.35), calls=%async_computation.4 | async-start | bytes 1441792 | tf_op jit(solution)/shard_map/all_to_all | solution.py:746
  345.3 5.2 %copy-start.34 = (f32[8,32,512]{2,1,0:T(8,128)}, f32[8,32,512]{2,1,0:T(8,128)S(1)}, u32[]{:S(2)}) copy-start(f32[8,32,512]{2,1,0:T(8,128)S(1)} %slice_convert_fusion.2) | copy-start | bytes 1572868
  352.3 5.1 %copy-start.1 = (s32[1,1024]{1,0:T(1,128)S(1)}, s32[1,1024]{1,0:T(1,128)}, u32[]{:S(2)}) copy-start(s32[1,1024]{1,0:T(1,128)} %param.24) | copy-start | bytes 12292
  (53 other events, 116.9 us)
Sparse Core Ops, SparseCore 0:
  48.0 31.7 all-gather.6
  115.5 35.4 all-gather.4
  225.6 22.2 reduce-scatter.10
  256.0 27.4 reduce-scatter.4
  285.6 33.9 reduce-scatter.6
  322.3 20.7 reduce-scatter.8
